TPU v7x, 256 devices: a whole 4x4x8 slice. The times are simulated.
256 devices in a mesh: rep: 8 (over y_hi, x), exp: 32 (over y_lo, z, core).
Axes of the slice: x: 4, y: 4 (y_hi: 2, y_lo: 2; y = y_hi * 2 + y_lo), z: 8, core: 2. Of those that a mesh axis runs over, the one named last changes fastest.
Arguments:
- features: bfloat16 [32768, 2048], P(('rep', 'exp')), may hold values from -6 to 6
- out_grad: bfloat16 [32768, 2048], P(('rep', 'exp')), may hold values from -1.5 to 1.5
- expert_ids: int32 [32768, 2], P(('rep', 'exp')), may hold values from 0 to 31, all different within a row; in each aligned block of 128 rows (0 to 127, 128 to 255, ...) at most 16 rows name the same one
- gate_probs: bfloat16 [32768, 2], P(('rep', 'exp')), may hold values from 0.049804688 to 0.59765625
- w_gate: bfloat16 [32, 2048, 768], P('exp'), may hold values from -0.125 to 0.125
- w_up: bfloat16 [32, 2048, 768], P('exp'), may hold values from -0.125 to 0.125
- w_down: bfloat16 [32, 2048, 768], P('exp'), may hold values from -0.21875 to 0.21875
Outputs:
- in_grad: bfloat16 [32768, 2048], P(('rep', 'exp'))
- gate_grad: bfloat16 [32768, 2], P(('rep', 'exp'))
- delta_gate: bfloat16 [32, 2048, 768], P('exp', 'rep')
- delta_up: bfloat16 [32, 2048, 768], P('exp', 'rep')
- delta_down: bfloat16 [32, 2048, 768], P('exp', 'rep')
Inputs may be any that keep to these rules, and one draw needn't show every extreme that they name: `expert_ids`: the 2 entries of a token name different experts. Among the 128 tokens of one device (aligned blocks in token order) no expert is named by more than 16 entries, and in every draw some expert is named by exactly 16 entries of some device. Every expert is named somewhere.
All inputs are finite; a program needn't handle non-finite values.
Results may differ from a plain program's by a relative error of at most 0.012.
Values may be sent and summed in bfloat16 or wider, within the bound.
A program may use at most 128 MiB of HBM per device.

v0:
```python
import jax
import jax.numpy as jnp
from jax import lax
from jax.sharding import PartitionSpec as P


def dot_rows(matrix_a, matrix_b):
    return lax.dot_general(
        matrix_a, matrix_b, (((0,), (0,)), ((), ())), preferred_element_type=jnp.float32
    )


def dot_last(matrix_a, matrix_b):
    return lax.dot_general(
        matrix_a, matrix_b, (((1,), (1,)), ((), ())), preferred_element_type=jnp.float32
    )


def expert_terms(inputs, gate_mat, up_mat, down_mat):
    rows_x, rows_dy, rows_g = inputs
    pre_gate = jnp.dot(rows_x, gate_mat, preferred_element_type=jnp.float32)
    pre_up = jnp.dot(rows_x, up_mat, preferred_element_type=jnp.float32)
    gate_sig = jax.nn.sigmoid(pre_gate)
    gate_act = pre_gate * gate_sig
    hidden = (gate_act * pre_up).astype(jnp.bfloat16)
    back_grad = jnp.dot(rows_dy, down_mat, preferred_element_type=jnp.float32)
    gate_row = jnp.sum(back_grad * hidden.astype(jnp.float32), axis=1).astype(jnp.bfloat16)
    scaled = (rows_g * rows_dy.astype(jnp.float32)).astype(jnp.bfloat16)
    d_hidden = rows_g * back_grad
    d_gate = (d_hidden * pre_up * gate_sig * (1.0 + pre_gate * (1.0 - gate_sig))).astype(
        jnp.bfloat16
    )
    d_up = (d_hidden * gate_act).astype(jnp.bfloat16)
    row_grad = (dot_last(d_gate, gate_mat) + dot_last(d_up, up_mat)).astype(jnp.bfloat16)
    return (row_grad, gate_row, hidden, scaled, d_gate, d_up)


def on_device(features, out_grad, expert_ids, gate_probs, w_gate, w_up, w_down):
    tokens, model_width = features.shape
    top_k = expert_ids.shape[1]
    hidden_units = w_gate.shape[2]
    experts = lax.axis_size("exp")
    replicas = lax.axis_size("rep")
    capacity = min(tokens, 2 * tokens * top_k // experts)
    flat_ids = expert_ids.reshape(-1)
    one_hot = (flat_ids[:, None] == jnp.arange(experts, dtype=jnp.int32)[None, :]).astype(jnp.int32)
    slot_index = jnp.sum((jnp.cumsum(one_hot, axis=0) - 1) * one_hot, axis=1)
    slot_count_all = experts * capacity
    target = flat_ids * capacity + slot_index
    entries = jnp.arange(tokens * top_k, dtype=jnp.int32)
    picked = jnp.zeros((slot_count_all,), jnp.int32).at[target].set(entries)
    filled = (
        jnp.zeros((slot_count_all,), jnp.bfloat16)
        .at[target]
        .set(jnp.ones((tokens * top_k,), jnp.bfloat16))
    )
    token_idx = picked // top_k
    keep = filled[:, None]
    send_x = (features[token_idx] * keep).reshape(experts, capacity, model_width)
    send_dy = (out_grad[token_idx] * keep).reshape(experts, capacity, model_width)
    send_g = (gate_probs.reshape(-1)[picked] * filled).reshape(experts, capacity)
    gate_mat, up_mat, down_mat = (w_gate[0], w_up[0], w_down[0])
    recv_x = lax.all_to_all(send_x, "exp", split_axis=0, concat_axis=0, tiled=True)
    recv_dy = lax.all_to_all(send_dy, "exp", split_axis=0, concat_axis=0, tiled=True)
    recv_g = lax.all_to_all(send_g, "exp", split_axis=0, concat_axis=0, tiled=True)
    senders, slot_count = recv_g.shape
    row_count = senders * slot_count
    inputs = (
        recv_x.reshape(row_count, model_width),
        recv_dy.reshape(row_count, model_width),
        recv_g.reshape(row_count, 1).astype(jnp.float32),
    )
    row_grad, gate_row, hidden, scaled, d_gate, d_up = expert_terms(
        inputs, gate_mat, up_mat, down_mat
    )
    outputs = (
        row_grad.reshape(senders, slot_count, model_width),
        gate_row.reshape(senders, slot_count),
        hidden.reshape(senders, slot_count, hidden_units),
        scaled.reshape(senders, slot_count, model_width),
        d_gate.reshape(senders, slot_count, hidden_units),
        d_up.reshape(senders, slot_count, hidden_units),
        recv_x,
    )
    returned = (
        lax.all_to_all(outputs[0], "exp", split_axis=0, concat_axis=0, tiled=True),
        lax.all_to_all(outputs[1], "exp", split_axis=0, concat_axis=0, tiled=True),
    )
    results = (returned[0], returned[1]) + outputs[2:]
    h_all = results[2].reshape(-1, hidden_units)
    a_all = results[3].reshape(-1, model_width)
    dg_all = results[4].reshape(-1, hidden_units)
    du_all = results[5].reshape(-1, hidden_units)
    x_all = results[6].reshape(-1, model_width)
    summed = lax.psum_scatter(
        jnp.concatenate(
            [dot_rows(x_all, dg_all), dot_rows(x_all, du_all), dot_rows(a_all, h_all)], axis=1
        ).astype(jnp.bfloat16),
        "rep",
        scatter_dimension=0,
        tiled=True,
    ).astype(jnp.float32)
    returned = (results[0], results[1])
    row_grads = (
        returned[0][flat_ids, slot_index].astype(jnp.float32).reshape(tokens, top_k, model_width)
    )
    in_grad = jnp.sum(row_grads, axis=1).astype(jnp.bfloat16)
    gate_grad = returned[1][flat_ids, slot_index].reshape(tokens, top_k)
    delta_gate = (summed[:, :hidden_units] / replicas).astype(jnp.bfloat16)[None]
    delta_up = (summed[:, hidden_units : 2 * hidden_units] / replicas).astype(jnp.bfloat16)[None]
    delta_down = (summed[:, 2 * hidden_units :] / replicas).astype(jnp.bfloat16)[None]
    return (in_grad, gate_grad, delta_gate, delta_up, delta_down)


def solution(mesh):
    in_specs = (
        P(("rep", "exp"), None),
        P(("rep", "exp"), None),
        P(("rep", "exp"), None),
        P(("rep", "exp"), None),
        P("exp", None, None),
        P("exp", None, None),
        P("exp", None, None),
    )
    out_specs = (
        P(("rep", "exp"), None),
        P(("rep", "exp"), None),
        P("exp", "rep", None),
        P("exp", "rep", None),
        P("exp", "rep", None),
    )
    return jax.shard_map(
        on_device, mesh=mesh, in_specs=in_specs, out_specs=out_specs, check_vma=False
    )
```

profile of v0, /device:TPU:1, one launch (start us, length us, event | category | flops | bytes accessed | tf_op | source)
XLA Modules:
  0.0 332.1 jit_solution(778370031099675027)
XLA Ops:
  9.5 1.4 scatter_custom_fusion
  11.9 2.2 scatter_custom_fusion.1
  14.1 3.4 %gather_fusion = bf16[512]{0:T(512)(128)(2,1)S(1)} fusion(bf16[256]{0:T(256)(128)(2,1)S(1)} %reshape.161, s32[1024]{0:T(1024)S(1)} %get-tuple-element.39), kind=kCustom, calls=%fused_computation | custom fusion | bytes 4096 | tf_op jit(solution)/shard_map/gather | solution.py:61
  18.1 11.1 %all-to-all-start = ((bf16[32,1,16]{2,1,0:T(2,128)(2,1)}), bf16[32,1,16]{2,1,0:T(2,128)(2,1)S(1)}, u32[]{:S(2)}, u32[]{:S(2)}) async-start(bf16[32,1,16]{2,1,0:T(2,128)(2,1)} %all_to_all.28), calls=%async_computation | async-start | bytes 32768 | tf_op jit(solution)/shard_map/all_to_all | solution.py:65
  29.4 6.4 %gather_fusion.1 = bf16[512,2048]{1,0:T(8,128)(2,1)} fusion(bf16[128,2048]{1,0:T(8,128)(2,1)} %param.8, s32[1024]{0:T(1024)S(1)} %get-tuple-element.38), kind=kCustom, calls=%fused_computation.1 | custom fusion | bytes 4196352 | tf_op jit(solution)/shard_map/gather | solution.py:60
  35.8 6.3 %gather_fusion.2 = bf16[512,2048]{1,0:T(8,128)(2,1)} fusion(bf16[128,2048]{1,0:T(8,128)(2,1)} %param.7, s32[1024]{0:T(1024)S(1)} %get-tuple-element.38), kind=kCustom, calls=%fused_computation.2 | custom fusion | bytes 4196352 | tf_op jit(solution)/shard_map/gather | solution.py:59
  42.1 4.6 %broadcast_multiply_fusion.1 = (bf16[32,16,2048]{2,1,0:T(8,128)(2,1)}, bf16[32,16,2048]{2,1,0:T(8,128)(2,1)}) fusion(bf16[32,16,2048]{2,1,0:T(8,128)(2,1)} %bitcast.60, bf16[32,16]{1,0:T(8,128)(2,1)S(1)} %mul.78, bf16[32,16,2048]{2,1,0:T(8,128)(2,1)} %bitcast.61), kind=kLoop, calls=%fused_computation.31 | loop fusion | flops 2097152 | bytes 8389632 | tf_op jit(solution)/shard_map/mul | solution.py:60
  46.7 57.4 %all_to_all.34 = bf16[32,16,2048]{2,1,0:T(8,128)(2,1)} all-to-all(bf16[32,16,2048]{2,1,0:T(8,128)(2,1)} %get-tuple-element.33), channel_id=1, replica_groups=mesh['rep'=8,'exp'=32] {'exp'}, dimensions={0} | all-to-all | bytes 4194304 | tf_op jit(solution)/shard_map/all_to_all | solution.py:63
  104.1 6.5 %all-to-all-start.1 = ((bf16[32,16,2048]{2,1,0:T(8,128)(2,1)}), bf16[32,16,2048]{2,1,0:T(8,128)(2,1)}, u32[]{:S(2)}, u32[]{:S(2)}) async-start(bf16[32,16,2048]{2,1,0:T(8,128)(2,1)} %get-tuple-element.32), calls=%async_computation.1 | async-start | bytes 4194304 | tf_op jit(solution)/shard_map/all_to_all | solution.py:64
  111.0 5.6 %fusion.6 = f32[512,768]{1,0:T(8,128)} fusion(bf16[512,2048]{1,0:T(8,128)(2,1)} %bitcast.62, bf16[1,2048,768]{2,1,0:T(8,128)(2,1)} %param.12), kind=kOutput, calls=%fused_computation.19 | convolution fusion | flops 1610612736 | bytes 6815744 | tf_op jit(solution)/shard_map/dot_general | solution.py:22
  116.6 3.0 fusion.2
  119.6 40.4 %all-to-all-done.1 = bf16[32,16,2048]{2,1,0:T(8,128)(2,1)} async-done(((bf16[32,16,2048]{2,1,0:T(8,128)(2,1)}), bf16[32,16,2048]{2,1,0:T(8,128)(2,1)}, u32[]{:S(2)}, u32[]{:S(2)}) %all-to-all-start.1) | async-done | bytes 2097184 | tf_op jit(solution)/shard_map/all_to_all | solution.py:64
  160.0 5.8 %multiply_reduce_fusion = (bf16[512]{0:T(512)(128)(2,1)S(1)}, bf16[512,768]{1,0:T(8,128)(2,1)S(1)}, bf16[512,768]{1,0:T(8,128)(2,1)S(1)}, bf16[512,768]{1,0:T(8,128)(2,1)S(1)}) fusion(f32[512,768]{1,0:T(8,128)} %fusion.6, f32[512,768]{1,0:T(8,128)} %fusion.2, f32[512]{0:T(512)S(1)} %reshape.168, bf16[512,2048]{1,0:T(8,128)(2,1)} %bitcast.4, ...), kind=kOutput, calls=%fused_computation.24 | convolution fusion | flops 1618083328 | bytes 10750976 | tf_op jit(solution)/shard_map/dot_general | solution.py:26
  165.9 4.1 %convolution_convert_fusion = bf16[2048,768]{0,1:T(8,128)(2,1)S(1)} fusion(bf16[512,768]{1,0:T(8,128)(2,1)S(1)} %get-tuple-element.26, bf16[512,2048]{1,0:T(8,128)(2,1)} %bitcast.4, f32[512]{0:T(512)S(1)} %reshape.168), kind=kOutput, calls=%fused_computation.10 | convolution fusion | flops 1615331328 | bytes 6031360 | tf_op jit(solution)/shard_map/dot_general | solution.py:8
  170.0 1.9 convolution_convert_fusion.1
  171.9 1.9 convolution_convert_fusion.2
  173.8 4.5 %pad_maximum_fusion = bf16[2048,2304]{0,1:T(8,128)(2,1)} fusion(bf16[2048,768]{0,1:T(8,128)(2,1)S(1)} %convolution_convert_fusion, bf16[2048,768]{0,1:T(8,128)(2,1)S(1)} %convolution_convert_fusion.1, bf16[2048,768]{0,1:T(8,128)(2,1)S(1)} %convolution_convert_fusion.2), kind=kLoop, calls=%fused_computation.7 | loop fusion | flops 28311552 | bytes 18874368 | tf_op jit(solution)/shard_map/concatenate | solution.py:96
  179.0 5.6 %all-to-all-start.4 = ((bf16[32,1,16]{2,1,0:T(2,128)(2,1)}), bf16[32,1,16]{2,1,0:T(2,128)(2,1)S(1)}, u32[]{:S(2)}, u32[]{:S(2)}) async-start(bf16[32,1,16]{2,1,0:T(2,128)(2,1)} %convert_element_type.84), calls=%async_computation.4 | async-start | bytes 32768 | tf_op jit(solution)/shard_map/all_to_all | solution.py:87
  184.7 3.1 fusion
  187.8 3.3 add_convert_fusion
  191.0 1.4 all-to-all-done.4
  192.4 7.0 %all-to-all-start.3 = ((bf16[32,16,2048]{2,1,0:T(8,128)(2,1)}), bf16[32,16,2048]{2,1,0:T(8,128)(2,1)}, u32[]{:S(2)}, u32[]{:S(2)}) async-start(bf16[32,16,2048]{2,1,0:T(8,128)(2,1)} %bitcast.66), calls=%async_computation.3 | async-start | bytes 4194304 | tf_op jit(solution)/shard_map/all_to_all | solution.py:86
  199.5 2.4 gather_fusion.4
  202.7 46.0 %all-to-all-done.3 = bf16[32,16,2048]{2,1,0:T(8,128)(2,1)} async-done(((bf16[32,16,2048]{2,1,0:T(8,128)(2,1)}), bf16[32,16,2048]{2,1,0:T(8,128)(2,1)}, u32[]{:S(2)}, u32[]{:S(2)}) %all-to-all-start.3) | async-done | bytes 2097184 | tf_op jit(solution)/shard_map/all_to_all | solution.py:86
  248.7 5.1 %gather_fusion.3 = bf16[256,2048]{1,0:T(8,128)(2,1)} fusion(bf16[32,16,2048]{2,1,0:T(8,128)(2,1)} %all-to-all-done.3, s32[256]{0:T(256)S(1)} %bitcast.59), kind=kCustom, calls=%fused_computation.3 | custom fusion | bytes 2099200 | tf_op jit(solution)/shard_map/gather | solution.py:105
  253.9 2.6 gather.27
  256.5 4.6 %reduce_sum.34 = bf16[128,2048]{1,0:T(8,128)(2,1)} reduce(bf16[128,2,2048]{2,1,0:T(2,128)(2,1)} %gather.27, bf16[]{:T(256)} %constant.39.clone.1), dimensions={1}, to_apply=%region_5.6 | reduce | flops 262144 | bytes 1572866 | tf_op jit(solution)/shard_map/reduce_sum | solution.py:107
  261.1 57.0 %reduce-scatter.2.cloned.1.call-done = bf16[256,2304]{0,1:T(8,128)(2,1)} async-done(((bf16[2048,2304]{0,1:T(8,128)(2,1)}), bf16[256,2304]{0,1:T(8,128)(2,1)}) %reduce-scatter.2.cloned.1.call-update) | async-done | bytes 1179664 | tf_op jit(solution)/shard_map/reduce_scatter | solution.py:95
  318.0 1.4 convert_element_type.79
  319.5 1.1 fusion.19
  320.6 1.9 copy.45
  322.5 1.9 copy.46
  (44 shorter events, 6.9 us)
Async XLA Ops:
  7.2 109.4 %copy-start = (bf16[1,2048,768]{2,1,0:T(8,128)(2,1)S(1)}, bf16[1,2048,768]{2,1,0:T(8,128)(2,1)}, u32[]{:S(2)}) copy-start(bf16[1,2048,768]{2,1,0:T(8,128)(2,1)} %param.11) | copy-start | bytes 9437188
  18.1 28.5 %all-to-all-start = ((bf16[32,1,16]{2,1,0:T(2,128)(2,1)}), bf16[32,1,16]{2,1,0:T(2,128)(2,1)S(1)}, u32[]{:S(2)}, u32[]{:S(2)}) async-start(bf16[32,1,16]{2,1,0:T(2,128)(2,1)} %all_to_all.28), calls=%async_computation | async-start | bytes 32768 | tf_op jit(solution)/shard_map/all_to_all | solution.py:65
  104.1 56.0 %all-to-all-start.1 = ((bf16[32,16,2048]{2,1,0:T(8,128)(2,1)}), bf16[32,16,2048]{2,1,0:T(8,128)(2,1)}, u32[]{:S(2)}, u32[]{:S(2)}) async-start(bf16[32,16,2048]{2,1,0:T(8,128)(2,1)} %get-tuple-element.32), calls=%async_computation.1 | async-start | bytes 4194304 | tf_op jit(solution)/shard_map/all_to_all | solution.py:64
  110.6 207.4 %reduce-scatter.2.cloned.1.call-start = ((), (), s32[]{:S(2)}) async-start(), calls=%async_computation.6 | async-start | bytes 10616832 | tf_op jit(solution)/shard_map/reduce_scatter | solution.py:95
  111.0 5.6 %copy-start.1 = (bf16[32,16,2048]{2,1,0:T(8,128)(2,1)S(1)}, bf16[32,16,2048]{2,1,0:T(8,128)(2,1)}, u32[]{:S(2)}) copy-start(bf16[32,16,2048]{2,1,0:T(8,128)(2,1)} %all_to_all.34) | copy-start | bytes 6291460
  165.8 4.2 %copy-start.4 = (bf16[512,768]{1,0:T(8,128)(2,1)}, bf16[512,768]{1,0:T(8,128)(2,1)S(1)}, u32[]{:S(2)}) copy-start(bf16[512,768]{1,0:T(8,128)(2,1)S(1)} %get-tuple-element.28) | copy-start | bytes 2359300
  165.9 6.0 %copy-start.6 = (bf16[512,768]{1,0:T(8,128)(2,1)}, bf16[512,768]{1,0:T(8,128)(2,1)S(1)}, u32[]{:S(2)}) copy-start(bf16[512,768]{1,0:T(8,128)(2,1)S(1)} %get-tuple-element.27) | copy-start | bytes 2359300
  165.9 4.2 %copy-start.2 = (bf16[32,16,2048]{2,1,0:T(8,128)(2,1)S(1)}, bf16[32,16,2048]{2,1,0:T(8,128)(2,1)}, u32[]{:S(2)}) copy-start(bf16[32,16,2048]{2,1,0:T(8,128)(2,1)} %all_to_all.34) | copy-start | bytes 6291460
  179.0 13.4 %all-to-all-start.4 = ((bf16[32,1,16]{2,1,0:T(2,128)(2,1)}), bf16[32,1,16]{2,1,0:T(2,128)(2,1)S(1)}, u32[]{:S(2)}, u32[]{:S(2)}) async-start(bf16[32,1,16]{2,1,0:T(2,128)(2,1)} %convert_element_type.84), calls=%async_computation.4 | async-start | bytes 32768 | tf_op jit(solution)/shard_map/all_to_all | solution.py:87
  184.6 3.1 copy-start.3
  184.7 3.1 copy-start.5
  192.4 56.3 %all-to-all-start.3 = ((bf16[32,16,2048]{2,1,0:T(8,128)(2,1)}), bf16[32,16,2048]{2,1,0:T(8,128)(2,1)}, u32[]{:S(2)}, u32[]{:S(2)}) async-start(bf16[32,16,2048]{2,1,0:T(8,128)(2,1)} %bitcast.66), calls=%async_computation.3 | async-start | bytes 4194304 | tf_op jit(solution)/shard_map/all_to_all | solution.py:86
Sparse Core Ops, SparseCore 0:
  178.4 139.5 reduce-scatter.1
where the time goes:
time: 333 us; the launch traced here: 332 us
  waiting for transfers between devices  145 us (44%)
  blocking collectives  57.4 us (17%)
  local copies, waits for them, and re-layouts  39.5 us (12%)
  starting transfers between devices  30.5 us (9%)
  matrix products  28.7 us (9%)
  other arithmetic  17 us (5%)
  between operations  14.3 us (4%)
    all_to_all x1, blocking collectives, on_device(): lax.all_to_all(send_x, 'exp', split_axis=0, concat_axis=0, tiled=True)  57.4 us
    reduce_scatter x1, waiting for transfers between devices, on_device(): lax.psum_scatter(jnp.concatenate([dot_rows(x_all, dg_all), dot_rows(x_all...  57 us
    all_to_all x1, waiting for transfers between devices, on_device(): lax.all_to_all(outputs[0], 'exp', split_axis=0, concat_axis=0, tiled=True)  46 us
    all_to_all x1, waiting for transfers between devices, on_device(): lax.all_to_all(send_dy, 'exp', split_axis=0, concat_axis=0, tiled=True)  40.4 us
    all_to_all x1, starting transfers between devices, on_device(): lax.all_to_all(send_g, 'exp', split_axis=0, concat_axis=0, tiled=True)  11.1 us
    dot_general x3, matrix products, dot_rows(): lax.dot_general(matrix_a, matrix_b, (((0,), (0,)), ((), ())), preferred_e...  7.87 us
    gather x2, local copies, waits for them, and re-layouts, on_device(): returned[0][flat_ids, slot_index].astype(jnp.float32)  7.73 us
    unnamed x20, local copies, waits for them, and re-layouts  7.11 us
  transfers between devices with their start and end apart: 5, of which 4 were waited for; matrix products, arithmetic and copies ran while one was open for 15% of the time, Pallas kernels for 0%

commit v1 on v0

v1 whole, which is shorter than its diff:
```python
import functools

import jax
import jax.numpy as jnp
from jax import lax
from jax.experimental import pallas as pl
from jax.experimental.pallas import tpu as pltpu
from jax.sharding import PartitionSpec as P

MESH = pl.DeviceIdType.MESH
F32 = jnp.float32
BF16 = jnp.bfloat16
TOK = 128
D = 2048
FF = 768
CAP = 16
NCH = 8
CW = D // NCH
SLOTS = 512
QS = ((0, 0), (0, 1), (1, 0), (1, 1))
BLOCKS = tuple(
    [(dy, dz, dc) for dy, dc in QS for dz in (0, -1, 1, -2, 2)]
    + [(dy, -3, dc) for dy, dc in QS]
    + [(dy, 3, dc) for dy, dc in QS]
    + [(0, 4, dc) for dc in (0, 1)]
    + [(1, 4, dc) for dc in (0, 1)]
)


def kernel(
    feat, og, meta, ids_col, wg, wu, wd,
    ig_out, gg_out, dl_out,
    src, msrc, s1, s2, stg1, stg2, stg3, stg4, gs1, gs2, gs3, gs4, rbuf, gbuf,
    wbuf, acc, acts, rg, ret, a2, ap, am, a0, rp, rm, ysend, yrecv,
    load_sem, w_sem, m_send, m_recv, ring_send, r1, r2, st_send, rx, gsend, grecv,
    a2_send, d_send, c_send, rp_sem, rm_sem, y_send, y_sem, ret_send, ret_sem,
):
    rep = lax.axis_index("rep")
    exp = lax.axis_index("exp")
    x = lax.rem(rep, 4)
    yh = rep // 4
    yl = exp // 16
    z = lax.rem(exp // 2, 8)
    c = lax.rem(exp, 2)

    def exp_of(dy, dz, dc):
        return lax.rem(yl + dy, 2) * 16 + lax.rem(z + dz + 8, 8) * 2 + lax.rem(c + dc, 2)

    def near(dy, dz, dc):
        return {"rep": rep, "exp": exp_of(dy, dz, dc)}

    xp = {"rep": yh * 4 + lax.rem(x + 1, 4), "exp": exp}
    xm = {"rep": yh * 4 + lax.rem(x + 3, 4), "exp": exp}
    yo = {"rep": (1 - yh) * 4 + x, "exp": exp}

    def send(a, b, ss, rs, to):
        pltpu.make_async_remote_copy(
            src_ref=a, dst_ref=b, send_sem=ss, recv_sem=rs, device_id=to, device_id_type=MESH
        ).start()

    def local(a, b, sem):
        pltpu.make_async_copy(a, b, sem).start()

    def wait(ref, sem):
        pltpu.make_async_copy(ref, ref, sem).wait()

    for k in range(NCH):
        cols = pl.ds(k * CW, CW)
        local(feat.at[:, cols], src.at[0, k, :, pl.ds(0, CW)], load_sem.at[k])
        local(og.at[:, cols], src.at[0, k, :, pl.ds(CW, CW)], load_sem.at[k])
    for m, w in enumerate((wg, wu, wd)):
        local(w.at[0], wbuf.at[m], w_sem.at[m])

    barrier = pltpu.get_barrier_semaphore()
    peers = [near(*b) for b in BLOCKS if b != (0, 0, 0)] + [xp, xm, yo]
    for p in peers:
        pl.semaphore_signal(barrier, inc=1, device_id=p, device_id_type=MESH)
    pl.semaphore_wait(barrier, len(peers))

    up, down = near(0, 1, 0), near(0, -1, 0)
    send(meta, msrc.at[0], m_send.at[0], m_recv.at[0], up)
    send(meta, msrc.at[1], m_send.at[1], m_recv.at[1], down)
    for k in range(NCH):
        wait(src.at[0, k], load_sem.at[k])
        send(src.at[0, k], src.at[1, k], ring_send.at[0], r1.at[0, k], up)
        send(src.at[0, k], src.at[2, k], ring_send.at[1], r1.at[1, k], down)

    row_i = lax.broadcasted_iota(jnp.int32, (TOK, TOK), 0)
    col_i = lax.broadcasted_iota(jnp.int32, (TOK, TOK), 1)
    before = jnp.where(row_i < col_i, 1.0, 0.0).astype(BF16)
    slot_i = lax.broadcasted_iota(jnp.int32, (CAP, TOK), 0).astype(F32)

    def pick(meta_v, experts):
        i0, i1, g0, g1 = [jnp.broadcast_to(meta_v[i : i + 1, :], (CAP, TOK)) for i in range(4)]
        rows, gates = [], []
        for e in experts:
            ef = e.astype(F32)
            m0, m1 = i0 == ef, i1 == ef
            hit = jnp.where(m0 | m1, 1.0, 0.0)
            pos = jnp.dot(hit.astype(BF16), before, preferred_element_type=F32)
            one = jnp.where(pos == slot_i, hit, 0.0)
            gate = jnp.sum(one * jnp.where(m0, g0, jnp.where(m1, g1, 0.0)), axis=1, keepdims=True)
            rows.append(one.astype(BF16))
            gates.append(jnp.broadcast_to(gate, (CAP, TOK)).astype(BF16))
        return rows, gates

    own_plane = [exp_of(dy, 0, dc) for dy, dc in QS]

    def plan_first(s, meta_v):
        rows, gates = pick(meta_v, own_plane)
        for q in range(4):
            s1[s, pl.ds(q * CAP, CAP), :] = rows[q]
            gs1[q, pl.ds(s * CAP, CAP), :] = gates[q]

    plan_first(0, meta[...])
    wait(msrc.at[0], m_recv.at[0])
    send(msrc.at[0], msrc.at[2], m_send.at[2], m_recv.at[2], up)
    wait(msrc.at[1], m_recv.at[1])
    send(msrc.at[1], msrc.at[3], m_send.at[3], m_recv.at[3], down)
    plan_first(1, msrc[0])
    plan_first(2, msrc[1])

    def first(k, carry):
        wait(src.at[1, k], r1.at[0, k])
        send(src.at[1, k], src.at[3, k], ring_send.at[2], r2.at[0, k], up)
        wait(src.at[2, k], r1.at[1, k])
        send(src.at[2, k], src.at[4, k], ring_send.at[3], r2.at[1, k], down)
        for s in range(3):
            got = jnp.dot(s1[s], src[s, k], preferred_element_type=F32).astype(BF16)
            for q in range(4):
                stg1[q, k, pl.ds(s * CAP, CAP), :] = got[q * CAP : (q + 1) * CAP]
        local(stg1.at[0, k], rbuf.at[k, pl.ds(0, 48)], rx.at[k])
        for q in range(1, 4):
            send(stg1.at[q, k], rbuf.at[k, pl.ds(q * 80, 48)], st_send.at[0], rx.at[k], near(QS[q][0], 0, QS[q][1]))
        return carry

    lax.fori_loop(0, NCH, first, 0)

    for d in range(2):
        step = 1 if d == 0 else -1
        wait(msrc.at[2 + d], m_recv.at[2 + d])
        third = [exp_of(dy, step, dc) for dy, dc in QS]
        fourth = [exp_of(d, 2 * step, dc) for dc in (0, 1)]
        rows, gates = pick(msrc[2 + d], own_plane + third + fourth)
        for i in range(10):
            s2[d, pl.ds(i * CAP, CAP), :] = rows[i]
        for q in range(4):
            gs2[q, pl.ds(d * CAP, CAP), :] = gates[q]
            gs3[d, q] = gates[4 + q]
        for i in range(2):
            gs4[d, i] = gates[8 + i]

    def second(k, carry):
        for d in range(2):
            step = 1 if d == 0 else -1
            wait(src.at[3 + d, k], r2.at[d, k])
            got = jnp.dot(s2[d], src[3 + d, k], preferred_element_type=F32).astype(BF16)
            for q in range(4):
                stg3[d, q, k] = got[(4 + q) * CAP : (5 + q) * CAP]
                stg2[q, k, pl.ds(d * CAP, CAP), :] = got[q * CAP : (q + 1) * CAP]
            for i in range(2):
                stg4[d, i, k] = got[(8 + i) * CAP : (9 + i) * CAP]
            for i in range(2):
                send(stg4.at[d, i, k], rbuf.at[k, pl.ds(448 + (d * 2 + i) * CAP, CAP)], st_send.at[3], rx.at[k], near(d, 2 * step, i))
            for q in range(4):
                send(stg3.at[d, q, k], rbuf.at[k, pl.ds(320 + (d * 4 + q) * CAP, CAP)], st_send.at[2], rx.at[k], near(QS[q][0], step, QS[q][1]))
        local(stg2.at[0, k], rbuf.at[k, pl.ds(48, 32)], rx.at[k])
        for q in range(1, 4):
            send(stg2.at[q, k], rbuf.at[k, pl.ds(q * 80 + 48, 32)], st_send.at[1], rx.at[k], near(QS[q][0], 0, QS[q][1]))
        return carry

    lax.fori_loop(0, NCH, second, 0)

    local(gs1.at[0], gbuf.at[pl.ds(0, 48)], grecv)
    local(gs2.at[0], gbuf.at[pl.ds(48, 32)], grecv)
    for q in range(1, 4):
        to = near(QS[q][0], 0, QS[q][1])
        send(gs1.at[q], gbuf.at[pl.ds(q * 80, 48)], gsend.at[0], grecv, to)
        send(gs2.at[q], gbuf.at[pl.ds(q * 80 + 48, 32)], gsend.at[1], grecv, to)
    for d in range(2):
        step = 1 if d == 0 else -1
        for q in range(4):
            send(gs3.at[d, q], gbuf.at[pl.ds(320 + (d * 4 + q) * CAP, CAP)], gsend.at[2], grecv, near(QS[q][0], step, QS[q][1]))
        for i in range(2):
            send(gs4.at[d, i], gbuf.at[pl.ds(448 + (d * 2 + i) * CAP, CAP)], gsend.at[3], grecv, near(d, 2 * step, i))

    for i in range(2):
        wait(src.at[0], ring_send.at[i])
        wait(src.at[1], ring_send.at[2 + i])
    for m in range(3):
        wait(wbuf.at[m], w_sem.at[m])
    wait(gbuf, grecv)

    def forward(k, carry):
        wait(rbuf.at[k], rx.at[k])
        krow = pl.ds(pl.multiple_of(k * CW, CW), CW)
        for m in range(3):
            a = rbuf[k, :, pl.ds(0 if m < 2 else CW, CW)]

            def tile(n, cc, m=m, a=a):
                ncol = pl.ds(pl.multiple_of(n * 256, 256), 256)
                part = jnp.dot(a, wbuf[m, krow, ncol], preferred_element_type=F32)

                @pl.when(k == 0)
                def _():
                    acc[m, :, ncol] = part

                @pl.when(k > 0)
                def _():
                    acc[m, :, ncol] = acc[m, :, ncol] + part

                return cc

            lax.fori_loop(0, FF // 256, tile, 0)
        gcol = gbuf[...].astype(F32)
        for h in range(2):
            src[h, k] = rbuf[k, :, pl.ds(h * TOK, TOK)].T
            dy = rbuf[k, :, pl.ds(CW + h * TOK, TOK)].astype(F32)
            src[2 + h, k] = (gcol * dy).astype(BF16).T
        return carry

    lax.fori_loop(0, NCH, forward, 0)

    def pointwise(i, carry):
        rows = pl.ds(pl.multiple_of(i * 32, 32), 32)
        g = gbuf[rows, pl.ds(0, 1)].astype(F32)
        pg, pu, bg = acc[0, rows, :], acc[1, rows, :], acc[2, rows, :]
        sig = jax.nn.sigmoid(pg)
        act = pg * sig
        hid = (act * pu).astype(BF16)
        gate = jnp.sum(bg * hid.astype(F32), axis=1, keepdims=True)
        dh = g * bg
        acts[0, rows, :] = (dh * pu * sig * (1.0 + pg * (1.0 - sig))).astype(BF16)
        acts[1, rows, :] = (dh * act).astype(BF16)
        acts[2, rows, :] = hid
        rg[rows, pl.ds(D, TOK)] = jnp.broadcast_to(gate, (32, TOK)).astype(BF16)
        return carry

    lax.fori_loop(0, SLOTS // 32, pointwise, 0)

    def product(owner, j):
        half, m = j // 3, lax.rem(j, 3)
        b = lax.rem(yh + 1 + half, 2) * 4 + lax.rem(x + owner, 4)
        w = (m // 2) * 2
        left = jnp.concatenate([src[w, b], src[w + 1, b]], axis=0)
        return jnp.dot(left, acts[m], preferred_element_type=F32).astype(BF16)

    def far(j, carry):
        v = product(2, j)
        a2[0, j] = v[:TOK]
        a2[1, j] = v[TOK:]
        send(a2.at[0, j], rp.at[0, j], a2_send.at[0], rp_sem.at[0, j], xm)
        send(a2.at[1, j], rm.at[0, j], a2_send.at[1], rm_sem.at[0, j], xp)
        return carry

    lax.fori_loop(0, 6, far, 0)

    def beside(j, carry):
        v = product(1, j)
        ap[0, j] = v[:TOK]
        ap[1, j] = v[TOK:]
        v = product(3, j)
        am[0, j] = v[:TOK]
        am[1, j] = v[TOK:]
        return carry

    lax.fori_loop(0, 6, beside, 0)

    def direct(j, carry):
        send(ap.at[0, j], rm.at[1, j], d_send.at[0], rm_sem.at[1, j], xp)
        send(am.at[1, j], rp.at[1, j], d_send.at[1], rp_sem.at[1, j], xm)
        return carry

    def combine(j, carry):
        wait(rm.at[0, j], rm_sem.at[0, j])
        ap[1, j] = (ap[1, j].astype(F32) + rm[0, j].astype(F32)).astype(BF16)
        send(ap.at[1, j], rm.at[2, j], c_send.at[0], rm_sem.at[2, j], xp)
        wait(rp.at[0, j], rp_sem.at[0, j])
        am[0, j] = (am[0, j].astype(F32) + rp[0, j].astype(F32)).astype(BF16)
        send(am.at[0, j], rp.at[2, j], c_send.at[1], rp_sem.at[2, j], xm)
        return carry

    lax.fori_loop(0, 3, direct, 0)

    def back(n, carry):
        nrow = pl.ds(pl.multiple_of(n * 256, 256), 256)
        dims = (((1,), (1,)), ((), ()))
        v = lax.dot_general(acts[0], wbuf[0, nrow, :], dims, preferred_element_type=F32)
        v = v + lax.dot_general(acts[1], wbuf[1, nrow, :], dims, preferred_element_type=F32)
        rg[:, nrow] = v.astype(BF16)
        return carry

    lax.fori_loop(0, D // 256, back, 0)
    for i, b in enumerate(BLOCKS):
        rows = pl.ds(i * CAP, CAP)
        if b == (0, 0, 0):
            local(rg.at[rows], ret.at[rows], ret_sem)
        else:
            send(rg.at[rows], ret.at[rows], ret_send, ret_sem, near(*b))

    lax.fori_loop(0, 3, combine, 0)
    lax.fori_loop(3, 6, direct, 0)

    def mine(j, carry):
        v = product(0, j)
        a0[0, j] = v[:TOK]
        a0[1, j] = v[TOK:]
        return carry

    lax.fori_loop(0, 6, mine, 0)
    lax.fori_loop(3, 6, combine, 0)

    def total(j, h):
        s = a0[h, j].astype(F32) + rp[2 - h, j].astype(F32)
        return s + rm[1 + h, j].astype(F32)

    def arrived(j):
        for i in (1, 2):
            wait(rp.at[i, j], rp_sem.at[i, j])
            wait(rm.at[i, j], rm_sem.at[i, j])

    def across(j, carry):
        arrived(j)
        for h in range(2):
            ysend[j, h] = total(j, h).astype(BF16)
        send(ysend.at[j], yrecv.at[j], y_send, y_sem.at[j], yo)
        return carry

    lax.fori_loop(0, 3, across, 0)

    wait(ret, ret_sem)
    lane = lax.broadcasted_iota(jnp.int32, (1, SLOTS), 1)
    blk = lane // CAP
    expert = jnp.zeros((1, SLOTS), F32)
    for i, (dy, dz, dc) in enumerate(BLOCKS):
        expert = jnp.where(blk == i, exp_of(dy, -dz, dc).astype(F32), expert)
    slot = (lane - blk * CAP).astype(F32)
    h0 = jnp.where(ids_col[:, 0:1] == expert, 1.0, 0.0)
    h1 = jnp.where(ids_col[:, 1:2] == expert, 1.0, 0.0)
    after = jnp.where(row_i > col_i, 1.0, 0.0).astype(BF16)
    pos = jnp.dot(after, (h0 + h1).astype(BF16), preferred_element_type=F32)
    h0 = jnp.where(pos == slot, h0, 0.0).astype(BF16)
    h1 = jnp.where(pos == slot, h1, 0.0).astype(BF16)
    both = h0 + h1

    def gather(n, carry):
        ncol = pl.ds(pl.multiple_of(n * 256, 256), 256)
        ig_out[:, ncol] = jnp.dot(both, ret[:, ncol], preferred_element_type=F32).astype(BF16)
        return carry

    lax.fori_loop(0, D // 256, gather, 0)
    g = ret[:, pl.ds(D, TOK)]
    g0 = jnp.dot(h0, g, preferred_element_type=F32)
    g1 = jnp.dot(h1, g, preferred_element_type=F32)
    gl = lax.broadcasted_iota(jnp.int32, (TOK, TOK), 1)
    gg_out[...] = jnp.where(gl == 0, g0, g1).astype(BF16)

    def finish(j, carry):
        arrived(j)
        wait(yrecv.at[j - 3], y_sem.at[j - 3])
        for h in range(2):
            s = total(j, h) + yrecv[j - 3, h].astype(F32)
            dl_out[j - 3, pl.ds(h * TOK, TOK), :] = (s * 0.125).astype(BF16)
        return carry

    lax.fori_loop(3, 6, finish, 0)

    for i in range(4):
        wait(msrc.at[0], m_send.at[i])
    wait(stg1.at[pl.ds(1, 3)], st_send.at[0])
    wait(stg2.at[pl.ds(1, 3)], st_send.at[1])
    wait(stg3, st_send.at[2])
    wait(stg4, st_send.at[3])
    wait(gs1.at[pl.ds(1, 3)], gsend.at[0])
    wait(gs2.at[pl.ds(1, 3)], gsend.at[1])
    wait(gs3, gsend.at[2])
    wait(gs4, gsend.at[3])
    for i in range(2):
        wait(a2.at[i], a2_send.at[i])
        wait(ap.at[i], d_send.at[i])
        wait(ap.at[i], c_send.at[i])
    wait(ysend, y_send)
    wait(rg.at[pl.ds(CAP, SLOTS - CAP)], ret_send)


def on_device(features, out_grad, expert_ids, gate_probs, w_gate, w_up, w_down):
    ids = expert_ids.astype(F32)
    meta = jnp.concatenate([ids.T, gate_probs.astype(F32).T, jnp.zeros((4, TOK), F32)], axis=0)
    vm, anyspace = pl.BlockSpec(memory_space=pltpu.VMEM), pl.BlockSpec(memory_space=pl.ANY)
    dma = pltpu.SemaphoreType.DMA
    ig, gg, dl = pl.pallas_call(
        kernel,
        name="moe",
        out_shape=(
            jax.ShapeDtypeStruct((TOK, D), BF16),
            jax.ShapeDtypeStruct((TOK, TOK), BF16),
            jax.ShapeDtypeStruct((3, 256, FF), BF16),
        ),
        in_specs=[anyspace, anyspace, vm, vm, anyspace, anyspace, anyspace],
        out_specs=(vm, vm, vm),
        scratch_shapes=[
            pltpu.VMEM((5, NCH, TOK, 2 * CW), BF16),
            pltpu.VMEM((4, 8, TOK), F32),
            pltpu.VMEM((3, 64, TOK), BF16),
            pltpu.VMEM((2, 160, TOK), BF16),
            pltpu.VMEM((4, NCH, 48, 2 * CW), BF16),
            pltpu.VMEM((4, NCH, 32, 2 * CW), BF16),
            pltpu.VMEM((2, 4, NCH, CAP, 2 * CW), BF16),
            pltpu.VMEM((2, 2, NCH, CAP, 2 * CW), BF16),
            pltpu.VMEM((4, 48, TOK), BF16),
            pltpu.VMEM((4, 32, TOK), BF16),
            pltpu.VMEM((2, 4, CAP, TOK), BF16),
            pltpu.VMEM((2, 2, CAP, TOK), BF16),
            pltpu.VMEM((NCH, SLOTS, 2 * CW), BF16),
            pltpu.VMEM((SLOTS, TOK), BF16),
            pltpu.VMEM((3, D, FF), BF16),
            pltpu.VMEM((3, SLOTS, FF), F32),
            pltpu.VMEM((3, SLOTS, FF), BF16),
            pltpu.VMEM((SLOTS, D + TOK), BF16),
            pltpu.VMEM((SLOTS, D + TOK), BF16),
            pltpu.VMEM((2, 6, TOK, FF), BF16),
            pltpu.VMEM((2, 6, TOK, FF), BF16),
            pltpu.VMEM((2, 6, TOK, FF), BF16),
            pltpu.VMEM((2, 6, TOK, FF), BF16),
            pltpu.VMEM((3, 6, TOK, FF), BF16),
            pltpu.VMEM((3, 6, TOK, FF), BF16),
            pltpu.VMEM((3, 2, TOK, FF), BF16),
            pltpu.VMEM((3, 2, TOK, FF), BF16),
            dma((NCH,)),
            dma((3,)),
            dma((4,)),
            dma((4,)),
            dma((4,)),
            dma((2, NCH)),
            dma((2, NCH)),
            dma((4,)),
            dma((NCH,)),
            dma((4,)),
            dma,
            dma((2,)),
            dma((2,)),
            dma((2,)),
            dma((3, 6)),
            dma((3, 6)),
            dma,
            dma((3,)),
            dma,
            dma,
        ],
        compiler_params=pltpu.CompilerParams(
            collective_id=0, has_side_effects=True, vmem_limit_bytes=67_000_000
        ),
    )(features, out_grad, meta, ids, w_gate, w_up, w_down)
    return (ig, gg[:, :2], dl[0:1], dl[1:2], dl[2:3])


def solution(mesh):
    rows = P(("rep", "exp"), None)
    weights = P("exp", None, None)
    deltas = P("exp", "rep", None)
    return jax.shard_map(
        on_device,
        mesh=mesh,
        in_specs=(rows, rows, rows, rows, weights, weights, weights),
        out_specs=(rows, rows, deltas, deltas, deltas),
        check_vma=False,
    )
```

time: 333 us -> 198 us (0.59)
  Pallas kernels: 0 us -> 189 us
  waiting for transfers between devices: 145 us -> 0 us
  blocking collectives: 57.4 us -> 0 us
  local copies, waits for them, and re-layouts: 39.5 us -> 6.41 us
  starting transfers between devices: 30.5 us -> 0 us
  matrix products: 28.7 us -> 0 us
  other arithmetic: 17 us -> 1.98 us
  between operations: 14.3 us -> 0.65 us
    pallas_call x0 -> x1, Pallas kernels: none -> 189 us  [on_device(): pl.pallas_call(kernel, name='moe', out_shape=(jax.ShapeDtypeStruct((TOK,...]
    all_to_all x4 -> x0, waiting for transfers between devices: 87.8 us -> none  [the longest x1 46 us: on_device(): lax.all_to_all(outputs[0], 'exp', split_axis=0, concat_axis=0, tiled=True)]
    all_to_all x1 -> x0, blocking collectives: 57.4 us -> none  [on_device(): lax.all_to_all(send_x, 'exp', split_axis=0, concat_axis=0, tiled=True)]
    reduce_scatter x1 -> x0, waiting for transfers between devices: 57 us -> none  [on_device(): lax.psum_scatter(jnp.concatenate([dot_rows(x_all, dg_all), dot_rows(x_all...]
    all_to_all x4 -> x0, starting transfers between devices: 30.3 us -> none  [the longest x1 11.1 us: on_device(): lax.all_to_all(send_g, 'exp', split_axis=0, concat_axis=0, tiled=True)]
    dot_general x8 -> x0, matrix products: 28.7 us -> none  [the longest x3 7.87 us: dot_rows(): lax.dot_general(matrix_a, matrix_b, (((0,), (0,)), ((), ())), preferred_e...]
    gather x6 -> x0, local copies, waits for them, and re-layouts: 26.3 us -> none  [the longest x2 7.73 us: on_device(): returned[0][flat_ids, slot_index].astype(jnp.float32)]
    reduce_sum x2 -> x0, other arithmetic: 4.71 us -> none  [the longest x1 4.61 us: on_device(): in_grad = jnp.sum(row_grads, axis=1).astype(jnp.bfloat16)]
  transfers between devices with their start and end apart: 5 -> 0, of which waited for: 4 -> 0; matrix products, arithmetic and copies ran while one was open for 15% -> 0% of each run, Pallas kernels for 0% -> 0%
where the time goes in v1:
time: 198 us
  Pallas kernels  189 us (95%)
  local copies, waits for them, and re-layouts  6.41 us (3%)
  other arithmetic  1.98 us (1%)
    pallas_call x1, Pallas kernels, on_device(): pl.pallas_call(kernel, name='moe', out_shape=(jax.ShapeDtypeStruct((TOK,...  189 us
    unnamed x3, local copies, waits for them, and re-layouts  4.01 us

profile of v1, /device:TPU:1, one launch (start us, length us, event | category | flops | bytes accessed | tf_op | source)
XLA Modules:
  0.0 198.0 jit_solution(13691207432985788450)
XLA Ops:
  0.6 0.1 pad.2.clone
  0.7 0.7 convert_bitcast_fusion
  1.4 0.8 copy.12
  2.2 0.6 fusion.1
  2.8 0.1 copy.13
  2.9 0.7 maximum_maximum_fusion.meta
  3.5 188.9 %moe.1 = (bf16[128,2048]{1,0:T(8,128)(2,1)}, bf16[128,128]{1,0:T(8,128)(2,1)}, bf16[3,256,768]{2,1,0:T(8,128)(2,1)}) custom-call(bf16[128,2048]{1,0:T(8,128)(2,1)} %feat.1, bf16[128,2048]{1,0:T(8,128)(2,1)} %og.1, f32[8,128]{1,0:T(8,128)} %maximum_maximum_fusion.meta, f32[128,2]{1,0:T(8,128)} %get-tuple-element.19.ids_col, bf16[1,2048,768]{2,1,0:T(8,128)(2,1)} %wg.1, ...), custom_call_target="tpu_custom_call" | custom-call | tf_op jit(solution)/shard_map/moe/pallas_call | solution.py:391
  192.5 1.4 copy.14
  193.8 2.3 %fusion = (bf16[1,256,768]{2,1,0:T(8,128)(2,1)}, bf16[1,256,768]{2,1,0:T(8,128)(2,1)}, bf16[1,256,768]{2,1,0:T(8,128)(2,1)}) fusion(bf16[3,256,768]{2,1,0:T(8,128)(2,1)} %get-tuple-element.10), kind=kLoop, calls=%fused_computation.3 | loop fusion | bytes 2359296 | tf_op jit(solution)/shard_map/slice | solution.py:454
  196.1 1.9 copy.16
  (1 shorter events, 0.0 us)

commit v2 on v1

v2 whole, which is shorter than its diff:
```python
import functools

import jax
import jax.numpy as jnp
from jax import lax
from jax.experimental import pallas as pl
from jax.experimental.pallas import tpu as pltpu
from jax.sharding import PartitionSpec as P

MESH = pl.DeviceIdType.MESH
F32 = jnp.float32
BF16 = jnp.bfloat16
TOK = 128
D = 2048
FF = 768
CAP = 16
NCH = 8
CW = D // NCH
SLOTS = 512
NEAR = 320
BW = 256
NA = 7
NB = 2
NU = 2 * NA + NB
QS = ((0, 0), (0, 1), (1, 0), (1, 1))
BLOCKS = tuple(
    [(dy, dz, dc) for dy, dc in QS for dz in (0, -1, 1, -2, 2)]
    + [(dy, -3, dc) for dy, dc in QS]
    + [(dy, 3, dc) for dy, dc in QS]
    + [(0, 4, dc) for dc in (0, 1)]
    + [(1, 4, dc) for dc in (0, 1)]
)


def kernel(
    feat, og, ids_row, gates_row, wg, wu, wd,
    ig_out, gg_out, dl_out,
    src, mine_meta, msrc, s1, s2, stg1, stg2, stg3, stg4, gs1, gs2, gs3, gs4, rbuf, gbuf,
    wbuf, acc, acts, rg, ret, a2, ap, am, a0, rp, rm, yb_send, yb_recv, ysend, yrecv,
    load_sem, w_sem, m_send, m_recv, ring_send, r1, r2, st_send, rx, rx2, gsend, grecv,
    a2_send, d_send, c_send, rp_sem, rm_sem, yb_ssem, yb_sem, y_send, y_sem, ret_send, ret_sem, hop_sem,
):
    rep = lax.axis_index("rep")
    exp = lax.axis_index("exp")
    x = lax.rem(rep, 4)
    yh = rep // 4
    yl = exp // 16
    z = lax.rem(exp // 2, 8)
    c = lax.rem(exp, 2)

    def exp_of(dy, dz, dc):
        return lax.rem(yl + dy, 2) * 16 + lax.rem(z + dz + 8, 8) * 2 + lax.rem(c + dc, 2)

    def near(dy, dz, dc):
        return {"rep": rep, "exp": exp_of(dy, dz, dc)}

    xp = {"rep": yh * 4 + lax.rem(x + 1, 4), "exp": exp}
    xm = {"rep": yh * 4 + lax.rem(x + 3, 4), "exp": exp}
    yo = {"rep": (1 - yh) * 4 + x, "exp": exp}

    def send(a, b, ss, rs, to):
        pltpu.make_async_remote_copy(
            src_ref=a, dst_ref=b, send_sem=ss, recv_sem=rs, device_id=to, device_id_type=MESH
        ).start()

    def local(a, b, sem):
        pltpu.make_async_copy(a, b, sem).start()

    def wait(ref, sem):
        pltpu.make_async_copy(ref, ref, sem).wait()

    for k in range(NCH):
        cols = pl.ds(k * CW, CW)
        local(feat.at[:, cols], src.at[0, k, :, pl.ds(0, CW)], load_sem.at[k])
        local(og.at[:, cols], src.at[0, k, :, pl.ds(CW, CW)], load_sem.at[k])
    for m, w in enumerate((wg, wu, wd)):
        local(w.at[0], wbuf.at[m], w_sem.at[m])

    mine_meta[...] = jnp.zeros_like(mine_meta)
    mine_meta[0:2, :] = ids_row[...].astype(F32)
    mine_meta[2:4, :] = gates_row[...].astype(F32)

    up, down = near(0, 1, 0), near(0, -1, 0)
    barrier = pltpu.get_barrier_semaphore()
    peers = [up, down] + [near(dy, 0, dc) for dy, dc in QS[1:]] + [xp, xm, yo]
    for p in peers:
        pl.semaphore_signal(barrier, inc=1, device_id=p, device_id_type=MESH)
    pl.semaphore_wait(barrier, len(peers))

    send(mine_meta, msrc.at[0], m_send.at[0], m_recv.at[0], up)
    send(mine_meta, msrc.at[1], m_send.at[1], m_recv.at[1], down)
    for k in range(NCH):
        wait(src.at[0, k], load_sem.at[k])
        send(src.at[0, k], src.at[1, k], ring_send.at[0], r1.at[0, k], up)
        send(src.at[0, k], src.at[2, k], ring_send.at[1], r1.at[1, k], down)

    def greet(i):
        for p in (up, down):
            pl.semaphore_signal(hop_sem.at[i], inc=1, device_id=p, device_id_type=MESH)

    def greeted(i):
        pl.semaphore_wait(hop_sem.at[i], 2)

    greet(0)
    row_i = lax.broadcasted_iota(jnp.int32, (TOK, TOK), 0)
    col_i = lax.broadcasted_iota(jnp.int32, (TOK, TOK), 1)
    before = jnp.where(row_i < col_i, 1.0, 0.0).astype(BF16)
    slot_i = lax.broadcasted_iota(jnp.int32, (CAP, TOK), 0).astype(F32)

    def pick(meta_v, experts):
        i0, i1, g0, g1 = [jnp.broadcast_to(meta_v[i : i + 1, :], (CAP, TOK)) for i in range(4)]
        rows, gates = [], []
        for e in experts:
            ef = e.astype(F32)
            m0, m1 = i0 == ef, i1 == ef
            hit = jnp.where(m0 | m1, 1.0, 0.0)
            pos = jnp.dot(hit.astype(BF16), before, preferred_element_type=F32)
            one = jnp.where(pos == slot_i, hit, 0.0)
            gate = jnp.sum(one * jnp.where(m0, g0, jnp.where(m1, g1, 0.0)), axis=1, keepdims=True)
            rows.append(one.astype(BF16))
            gates.append(jnp.broadcast_to(gate, (CAP, TOK)).astype(BF16))
        return rows, gates

    own_plane = [exp_of(dy, 0, dc) for dy, dc in QS]

    def plan_first(s, meta_v):
        rows, gates = pick(meta_v, own_plane)
        for q in range(4):
            s1[s, pl.ds(q * CAP, CAP), :] = rows[q]
            gs1[q, pl.ds(s * CAP, CAP), :] = gates[q]

    plan_first(0, mine_meta[...])
    for i in range(3):
        greeted(i)
        greet(i + 1)
    wait(msrc.at[0], m_recv.at[0])
    send(msrc.at[0], msrc.at[2], m_send.at[2], m_recv.at[2], up)
    wait(msrc.at[1], m_recv.at[1])
    send(msrc.at[1], msrc.at[3], m_send.at[3], m_recv.at[3], down)
    plan_first(1, msrc[0])
    plan_first(2, msrc[1])
    greeted(3)
    local(gs1.at[0], gbuf.at[pl.ds(0, 48)], grecv.at[0])
    for q in range(1, 4):
        send(gs1.at[q], gbuf.at[pl.ds(q * 80, 48)], gsend.at[0], grecv.at[0], near(QS[q][0], 0, QS[q][1]))

    def first(k, carry):
        wait(src.at[1, k], r1.at[0, k])
        send(src.at[1, k], src.at[3, k], ring_send.at[2], r2.at[0, k], up)
        wait(src.at[2, k], r1.at[1, k])
        send(src.at[2, k], src.at[4, k], ring_send.at[3], r2.at[1, k], down)
        for s in range(3):
            got = jnp.dot(s1[s], src[s, k], preferred_element_type=F32).astype(BF16)
            for q in range(4):
                stg1[q, k, pl.ds(s * CAP, CAP), :] = got[q * CAP : (q + 1) * CAP]
        local(stg1.at[0, k], rbuf.at[k, pl.ds(0, 48)], rx.at[k])
        for q in range(1, 4):
            send(stg1.at[q, k], rbuf.at[k, pl.ds(q * 80, 48)], st_send.at[0], rx.at[k], near(QS[q][0], 0, QS[q][1]))
        return carry

    lax.fori_loop(0, NCH, first, 0)

    for d in range(2):
        step = 1 if d == 0 else -1
        wait(msrc.at[2 + d], m_recv.at[2 + d])
        third = [exp_of(dy, step, dc) for dy, dc in QS]
        fourth = [exp_of(d, 2 * step, dc) for dc in (0, 1)]
        rows, gates = pick(msrc[2 + d], own_plane + third + fourth)
        for i in range(10):
            s2[d, pl.ds(i * CAP, CAP), :] = rows[i]
        for q in range(4):
            gs2[q, pl.ds(d * CAP, CAP), :] = gates[q]
            gs3[d, q] = gates[4 + q]
        for i in range(2):
            gs4[d, i] = gates[8 + i]
    local(gs2.at[0], gbuf.at[pl.ds(48, 32)], grecv.at[0])
    for q in range(1, 4):
        send(gs2.at[q], gbuf.at[pl.ds(q * 80 + 48, 32)], gsend.at[1], grecv.at[0], near(QS[q][0], 0, QS[q][1]))
    for d in range(2):
        step = 1 if d == 0 else -1
        for q in range(4):
            send(gs3.at[d, q], gbuf.at[pl.ds(320 + (d * 4 + q) * CAP, CAP)], gsend.at[2], grecv.at[1], near(QS[q][0], step, QS[q][1]))
        for i in range(2):
            send(gs4.at[d, i], gbuf.at[pl.ds(448 + (d * 2 + i) * CAP, CAP)], gsend.at[3], grecv.at[1], near(d, 2 * step, i))

    def second(k, carry):
        for d in range(2):
            step = 1 if d == 0 else -1
            wait(src.at[3 + d, k], r2.at[d, k])
            got = jnp.dot(s2[d], src[3 + d, k], preferred_element_type=F32).astype(BF16)
            for q in range(4):
                stg3[d, q, k] = got[(4 + q) * CAP : (5 + q) * CAP]
                stg2[q, k, pl.ds(d * CAP, CAP), :] = got[q * CAP : (q + 1) * CAP]
            for i in range(2):
                stg4[d, i, k] = got[(8 + i) * CAP : (9 + i) * CAP]
            for i in range(2):
                send(stg4.at[d, i, k], rbuf.at[k, pl.ds(448 + (d * 2 + i) * CAP, CAP)], st_send.at[3], rx2.at[k], near(d, 2 * step, i))
            for q in range(4):
                send(stg3.at[d, q, k], rbuf.at[k, pl.ds(320 + (d * 4 + q) * CAP, CAP)], st_send.at[2], rx2.at[k], near(QS[q][0], step, QS[q][1]))
        local(stg2.at[0, k], rbuf.at[k, pl.ds(48, 32)], rx.at[k])
        for q in range(1, 4):
            send(stg2.at[q, k], rbuf.at[k, pl.ds(q * 80 + 48, 32)], st_send.at[1], rx.at[k], near(QS[q][0], 0, QS[q][1]))
        return carry

    lax.fori_loop(0, NCH, second, 0)

    for i in range(2):
        wait(src.at[0], ring_send.at[i])
        wait(src.at[1], ring_send.at[2 + i])
    for m in range(3):
        wait(wbuf.at[m], w_sem.at[m])
    wait(gbuf.at[pl.ds(0, NEAR)], grecv.at[0])
    for k in range(NCH):
        wait(rbuf.at[k, pl.ds(0, NEAR)], rx.at[k])

    def near_rows(n, carry):
        ncol = pl.ds(pl.multiple_of(n * 256, 256), 256)
        for m in range(3):
            c0 = 0 if m < 2 else CW
            v = jnp.zeros((NEAR, 256), F32)
            for k in range(NCH):
                v = v + jnp.dot(
                    rbuf[k, pl.ds(0, NEAR), pl.ds(c0, CW)],
                    wbuf[m, pl.ds(k * CW, CW), ncol],
                    preferred_element_type=F32,
                )
            acc[m, pl.ds(0, NEAR), ncol] = v
        return carry

    lax.fori_loop(0, FF // 256, near_rows, 0)

    def turn(k, r0):
        rows = pl.ds(r0, 256)
        gcol = gbuf[rows, :].astype(F32)
        for h in range(2):
            src[h, k, :, rows] = rbuf[k, rows, pl.ds(h * TOK, TOK)].T
            dy = rbuf[k, rows, pl.ds(CW + h * TOK, TOK)].astype(F32)
            src[2 + h, k, :, rows] = (gcol * dy).astype(BF16).T

    def turn_first(k, carry):
        turn(k, 0)
        return carry

    lax.fori_loop(0, NCH, turn_first, 0)

    def pointwise(i, carry):
        rows = pl.ds(pl.multiple_of(i * 32, 32), 32)
        g = gbuf[rows, pl.ds(0, 1)].astype(F32)
        pg, pu, bg = acc[0, rows, :], acc[1, rows, :], acc[2, rows, :]
        sig = jax.nn.sigmoid(pg)
        act = pg * sig
        hid = (act * pu).astype(BF16)
        gate = jnp.sum(bg * hid.astype(F32), axis=1, keepdims=True)
        dh = g * bg
        d_gate = (dh * pu * sig * (1.0 + pg * (1.0 - sig))).astype(BF16)
        d_up = (dh * act).astype(BF16)
        for n in range(FF // BW):
            cols = slice(n * BW, (n + 1) * BW)
            acts[n, rows, :] = d_gate[:, cols]
            acts[3 + n, rows, :] = d_up[:, cols]
            acts[6 + n, rows, :] = hid[:, cols]
        rg[rows, pl.ds(D, TOK)] = jnp.broadcast_to(gate, (32, TOK)).astype(BF16)
        return carry

    lax.fori_loop(0, NEAR // 32, pointwise, 0)

    wait(gbuf.at[pl.ds(NEAR, SLOTS - NEAR)], grecv.at[1])
    rest = pl.ds(NEAR, SLOTS - NEAR)

    def far_rows(k, carry):
        wait(rbuf.at[k, rest], rx2.at[k])
        krow = pl.ds(pl.multiple_of(k * CW, CW), CW)
        for m in range(3):
            a = rbuf[k, rest, pl.ds(0 if m < 2 else CW, CW)]
            part = jnp.dot(a, wbuf[m, krow, :], preferred_element_type=F32)

            @pl.when(k == 0)
            def _():
                acc[m, rest, :] = part

            @pl.when(k > 0)
            def _():
                acc[m, rest, :] = acc[m, rest, :] + part

        turn(k, 256)
        return carry

    lax.fori_loop(0, NCH, far_rows, 0)
    lax.fori_loop(NEAR // 32, SLOTS // 32, pointwise, 0)

    def product(owner, half, n):
        b = lax.rem(yh + 1 + half, 2) * 4 + lax.rem(x + owner, 4)
        w = (n // 6) * 2
        left = jnp.concatenate([src[w, b], src[w + 1, b]], axis=0)
        return jnp.dot(left, acts[n], preferred_element_type=F32)

    def put(ref, u, v):
        v = v.astype(BF16)
        ref[0, u] = v[:TOK]
        ref[1, u] = v[TOK:]

    def send_far(u):
        send(a2.at[0, u], rp.at[0, u], a2_send.at[0], rp_sem.at[0, u], xm)
        send(a2.at[1, u], rm.at[0, u], a2_send.at[1], rm_sem.at[0, u], xp)

    def far(u, carry):
        put(a2, u, product(2, u // NA, lax.rem(u, NA)))
        send_far(u)
        return carry

    lax.fori_loop(0, 2 * NA, far, 0)

    def to_y(i, carry):
        o, n = i // NB, lax.rem(i, NB)
        yb_send[o, n] = product(o, 0, NA + n).astype(BF16)
        send(yb_send.at[o, n], yb_recv.at[o, n], yb_ssem, yb_sem, yo)
        return carry

    lax.fori_loop(0, 4 * NB, to_y, 0)

    def beside(u, carry):
        put(ap, u, product(1, u // NA, lax.rem(u, NA)))
        put(am, u, product(3, u // NA, lax.rem(u, NA)))
        return carry

    lax.fori_loop(0, 2 * NA, beside, 0)

    def direct(u, carry):
        send(ap.at[0, u], rm.at[1, u], d_send.at[0], rm_sem.at[1, u], xp)
        send(am.at[1, u], rp.at[1, u], d_send.at[1], rp_sem.at[1, u], xm)
        return carry

    def combine(u, carry):
        wait(rm.at[0, u], rm_sem.at[0, u])
        ap[1, u] = (ap[1, u].astype(F32) + rm[0, u].astype(F32)).astype(BF16)
        send(ap.at[1, u], rm.at[2, u], c_send.at[0], rm_sem.at[2, u], xp)
        wait(rp.at[0, u], rp_sem.at[0, u])
        am[0, u] = (am[0, u].astype(F32) + rp[0, u].astype(F32)).astype(BF16)
        send(am.at[0, u], rp.at[2, u], c_send.at[1], rp_sem.at[2, u], xm)
        return carry

    lax.fori_loop(0, NA, direct, 0)

    def back(n, carry):
        nrow = pl.ds(pl.multiple_of(n * 256, 256), 256)
        dims = (((1,), (1,)), ((), ()))
        v = jnp.zeros((SLOTS, 256), F32)
        for i in range(6):
            w = wbuf[i // 3, nrow, pl.ds((i % 3) * BW, BW)]
            v = v + lax.dot_general(acts[i], w, dims, preferred_element_type=F32)
        rg[:, nrow] = v.astype(BF16)
        return carry

    lax.fori_loop(0, D // 256, back, 0)
    for i, b in enumerate(BLOCKS):
        rows = pl.ds(i * CAP, CAP)
        if b == (0, 0, 0):
            local(rg.at[rows], ret.at[rows], ret_sem)
        else:
            send(rg.at[rows], ret.at[rows], ret_send, ret_sem, near(*b))

    lax.fori_loop(0, NA, combine, 0)
    lax.fori_loop(NA, 2 * NA, direct, 0)
    lax.fori_loop(NA, 2 * NA, combine, 0)

    def own(u, carry):
        put(a0, u, product(0, u // NA, lax.rem(u, NA)))
        return carry

    lax.fori_loop(0, 2 * NA, own, 0)

    wait(yb_recv, yb_sem)

    def y_first(n, carry):
        u = 2 * NA + n
        put(a2, u, product(2, 1, NA + n) + yb_recv[2, n].astype(F32))
        send_far(u)
        put(ap, u, product(1, 1, NA + n) + yb_recv[1, n].astype(F32))
        put(am, u, product(3, 1, NA + n) + yb_recv[3, n].astype(F32))
        return carry

    lax.fori_loop(0, NB, y_first, 0)
    lax.fori_loop(2 * NA, NU, direct, 0)

    def y_own(n, carry):
        put(a0, 2 * NA + n, product(0, 1, NA + n) + yb_recv[0, n].astype(F32))
        return carry

    lax.fori_loop(0, NB, y_own, 0)

    def total(u, h):
        s = a0[h, u].astype(F32) + rp[2 - h, u].astype(F32)
        return s + rm[1 + h, u].astype(F32)

    def arrived(u):
        for i in (1, 2):
            wait(rp.at[i, u], rp_sem.at[i, u])
            wait(rm.at[i, u], rm_sem.at[i, u])

    def across(u, carry):
        arrived(u)
        for h in range(2):
            ysend[u, h] = total(u, h).astype(BF16)
        send(ysend.at[u], yrecv.at[u], y_send, y_sem.at[u], yo)
        return carry

    lax.fori_loop(0, NA, across, 0)
    lax.fori_loop(2 * NA, NU, combine, 0)

    lane = lax.broadcasted_iota(jnp.int32, (1, SLOTS), 1)
    blk = lane // CAP
    expert = jnp.zeros((1, SLOTS), F32)
    for i, (dy, dz, dc) in enumerate(BLOCKS):
        expert = jnp.where(blk == i, exp_of(dy, -dz, dc).astype(F32), expert)
    slot = (lane - blk * CAP).astype(F32)
    ids_col = jnp.concatenate([mine_meta[...]] * (TOK // 8), axis=0).T
    h0 = jnp.where(ids_col[:, 0:1] == expert, 1.0, 0.0)
    h1 = jnp.where(ids_col[:, 1:2] == expert, 1.0, 0.0)
    after = jnp.where(row_i > col_i, 1.0, 0.0).astype(BF16)
    pos = jnp.dot(after, (h0 + h1).astype(BF16), preferred_element_type=F32)
    h0 = jnp.where(pos == slot, h0, 0.0).astype(BF16)
    h1 = jnp.where(pos == slot, h1, 0.0).astype(BF16)
    both = h0 + h1
    wait(ret, ret_sem)

    def gather(n, carry):
        ncol = pl.ds(pl.multiple_of(n * 256, 256), 256)
        ig_out[:, ncol] = jnp.dot(both, ret[:, ncol], preferred_element_type=F32).astype(BF16)
        return carry

    lax.fori_loop(0, D // 256, gather, 0)
    g = ret[:, pl.ds(D, TOK)]
    g0 = jnp.dot(h0, g, preferred_element_type=F32).T
    g1 = jnp.dot(h1, g, preferred_element_type=F32).T
    gg_out[...] = jnp.concatenate([g0[0:1], g1[0:1]], axis=0).astype(BF16)

    def finish(n, carry):
        u = NA + n
        arrived(u)
        wait(yrecv.at[n], y_sem.at[n])
        for h in range(2):
            s = total(u, h) + yrecv[n, h].astype(F32)
            dl_out[n, pl.ds(h * TOK, TOK), :] = (s * 0.125).astype(BF16)
        return carry

    lax.fori_loop(0, NA, finish, 0)

    def finish_y(n, carry):
        u = 2 * NA + n
        arrived(u)
        for h in range(2):
            dl_out[NA + n, pl.ds(h * TOK, TOK), :] = (total(u, h) * 0.125).astype(BF16)
        return carry

    lax.fori_loop(0, NB, finish_y, 0)

    for i in range(4):
        wait(mine_meta, m_send.at[i])
    wait(stg1.at[pl.ds(1, 3)], st_send.at[0])
    wait(stg2.at[pl.ds(1, 3)], st_send.at[1])
    wait(stg3, st_send.at[2])
    wait(stg4, st_send.at[3])
    wait(gs1.at[pl.ds(1, 3)], gsend.at[0])
    wait(gs2.at[pl.ds(1, 3)], gsend.at[1])
    wait(gs3, gsend.at[2])
    wait(gs4, gsend.at[3])
    for i in range(2):
        wait(a2.at[i], a2_send.at[i])
        wait(ap.at[i], d_send.at[i])
        wait(ap.at[i], c_send.at[i])
    wait(yb_send, yb_ssem)
    wait(ysend, y_send)
    wait(rg.at[pl.ds(CAP, SLOTS - CAP)], ret_send)


def place(ig, gg, dl, ig_out, gg_out, dg_out, du_out, dd_out):
    ig_out[...] = ig[...]
    gg_out[...] = gg[...]
    for n in range(FF // BW):
        cols = pl.ds(n * BW, BW)
        for m, ref in enumerate((dg_out, du_out, dd_out)):
            ref[0, :, cols] = dl[3 * m + n]


def on_device(features, out_grad, expert_ids, gate_probs, w_gate, w_up, w_down):
    vm, anyspace = pl.BlockSpec(memory_space=pltpu.VMEM), pl.BlockSpec(memory_space=pl.ANY)
    dma = pltpu.SemaphoreType.DMA
    ig, gg, dl = pl.pallas_call(
        kernel,
        name="moe",
        out_shape=(
            jax.ShapeDtypeStruct((TOK, D), BF16),
            jax.ShapeDtypeStruct((2, TOK), BF16),
            jax.ShapeDtypeStruct((9, 256, BW), BF16),
        ),
        in_specs=[anyspace, anyspace, vm, vm, anyspace, anyspace, anyspace],
        out_specs=(vm, vm, vm),
        scratch_shapes=[
            pltpu.VMEM((5, NCH, TOK, 2 * CW), BF16),
            pltpu.VMEM((8, TOK), F32),
            pltpu.VMEM((4, 8, TOK), F32),
            pltpu.VMEM((3, 64, TOK), BF16),
            pltpu.VMEM((2, 160, TOK), BF16),
            pltpu.VMEM((4, NCH, 48, 2 * CW), BF16),
            pltpu.VMEM((4, NCH, 32, 2 * CW), BF16),
            pltpu.VMEM((2, 4, NCH, CAP, 2 * CW), BF16),
            pltpu.VMEM((2, 2, NCH, CAP, 2 * CW), BF16),
            pltpu.VMEM((4, 48, TOK), BF16),
            pltpu.VMEM((4, 32, TOK), BF16),
            pltpu.VMEM((2, 4, CAP, TOK), BF16),
            pltpu.VMEM((2, 2, CAP, TOK), BF16),
            pltpu.VMEM((NCH, SLOTS, 2 * CW), BF16),
            pltpu.VMEM((SLOTS, TOK), BF16),
            pltpu.VMEM((3, D, FF), BF16),
            pltpu.VMEM((3, SLOTS, FF), F32),
            pltpu.VMEM((9, SLOTS, BW), BF16),
            pltpu.VMEM((SLOTS, D + TOK), BF16),
            pltpu.VMEM((SLOTS, D + TOK), BF16),
            pltpu.VMEM((2, NU, TOK, BW), BF16),
            pltpu.VMEM((2, NU, TOK, BW), BF16),
            pltpu.VMEM((2, NU, TOK, BW), BF16),
            pltpu.VMEM((2, NU, TOK, BW), BF16),
            pltpu.VMEM((3, NU, TOK, BW), BF16),
            pltpu.VMEM((3, NU, TOK, BW), BF16),
            pltpu.VMEM((4, NB, 256, BW), BF16),
            pltpu.VMEM((4, NB, 256, BW), BF16),
            pltpu.VMEM((NA, 2, TOK, BW), BF16),
            pltpu.VMEM((NA, 2, TOK, BW), BF16),
            dma((NCH,)),
            dma((3,)),
            dma((4,)),
            dma((4,)),
            dma((4,)),
            dma((2, NCH)),
            dma((2, NCH)),
            dma((4,)),
            dma((NCH,)),
            dma((NCH,)),
            dma((4,)),
            dma((2,)),
            dma((2,)),
            dma((2,)),
            dma((2,)),
            dma((3, NU)),
            dma((3, NU)),
            dma,
            dma,
            dma,
            dma((NA,)),
            dma,
            dma,
            pltpu.SemaphoreType.REGULAR((4,)),
        ],
        compiler_params=pltpu.CompilerParams(
            collective_id=0, has_side_effects=True, vmem_limit_bytes=67_000_000
        ),
    )(features, out_grad, expert_ids.T, gate_probs.T, w_gate, w_up, w_down)
    delta = jax.ShapeDtypeStruct((1, 256, FF), BF16)
    ig, gg, d_gate, d_up, d_down = pl.pallas_call(
        place,
        name="place",
        out_shape=(
            jax.ShapeDtypeStruct((TOK, D), BF16),
            jax.ShapeDtypeStruct((2, TOK), BF16),
            delta,
            delta,
            delta,
        ),
        in_specs=[vm] * 3,
        out_specs=(vm,) * 5,
    )(ig, gg, dl)
    return (ig, gg.T, d_gate, d_up, d_down)


def solution(mesh):
    rows = P(("rep", "exp"), None)
    weights = P("exp", None, None)
    deltas = P("exp", "rep", None)
    return jax.shard_map(
        on_device,
        mesh=mesh,
        in_specs=(rows, rows, rows, rows, weights, weights, weights),
        out_specs=(rows, rows, deltas, deltas, deltas),
        check_vma=False,
    )
```

time: 198 us -> 161 us (0.81)
  Pallas kernels: 189 us -> 160 us
  local copies, waits for them, and re-layouts: 6.41 us -> 0 us
  other arithmetic: 1.98 us -> 0 us
    pallas_call x1, Pallas kernels: 189 us -> 157 us  [on_device(): pl.pallas_call(kernel, name='moe', out_shape=(jax.ShapeDtypeStruct((TOK,...]
    unnamed x3 -> x0, local copies, waits for them, and re-layouts: 4.01 us -> none
    pallas_call x0 -> x1, Pallas kernels: none -> 2.65 us  [on_device(): pl.pallas_call(place, name='place', out_shape=(jax.ShapeDtypeStruct((TOK,...]
    slice x1 -> x0, local copies, waits for them, and re-layouts: 2.26 us -> none  [on_device(): return (ig, gg[:, :2], dl[0:1], dl[1:2], dl[2:3])]
where the time goes in v2:
time: 161 us
  Pallas kernels  160 us (99%)
    pallas_call x1, Pallas kernels, on_device(): pl.pallas_call(kernel, name='moe', out_shape=(jax.ShapeDtypeStruct((TOK,...  157 us

profile of v2, /device:TPU:1, one launch (start us, length us, event | category | flops | bytes accessed | tf_op | source)
XLA Modules:
  0.0 160.7 jit_solution(14803890980326195743)
XLA Ops:
  0.6 157.4 %moe.1 = (bf16[128,2048]{1,0:T(8,128)(2,1)}, bf16[2,128]{1,0:T(2,128)(2,1)}, bf16[9,256,256]{2,1,0:T(8,128)(2,1)}) custom-call(bf16[128,2048]{1,0:T(8,128)(2,1)} %feat.1, bf16[128,2048]{1,0:T(8,128)(2,1)} %og.1, s32[2,128]{1,0:T(2,128)} %bitcast.3, bf16[2,128]{1,0:T(2,128)(2,1)} %bitcast.4, bf16[1,2048,768]{2,1,0:T(8,128)(2,1)} %wg.1, ...), custom_call_target="tpu_custom_call" | custom-call | tf_op jit(solution)/shard_map/moe/pallas_call | solution.py:488
  158.0 2.6 %place.1 = (bf16[128,2048]{1,0:T(8,128)(2,1)}, bf16[2,128]{1,0:T(2,128)(2,1)}, bf16[1,256,768]{2,1,0:T(8,128)(2,1)}, bf16[1,256,768]{2,1,0:T(8,128)(2,1)}, bf16[1,256,768]{2,1,0:T(8,128)(2,1)}) custom-call(bf16[128,2048]{1,0:T(8,128)(2,1)} %get-tuple-element.13.ig, bf16[2,128]{1,0:T(2,128)(2,1)} %get-tuple-element.14.gg, ...), custom_call_target="tpu_custom_call" | custom-call | tf_op jit(solution)/shard_map/place/pallas_call | solution.py:559

commit v3 on v2

v3 whole, which is shorter than its diff:
```python
import functools

import jax
import jax.numpy as jnp
from jax import lax
from jax.experimental import pallas as pl
from jax.experimental.pallas import tpu as pltpu
from jax.sharding import PartitionSpec as P

MESH = pl.DeviceIdType.MESH
F32 = jnp.float32
BF16 = jnp.bfloat16
TOK = 128
D = 2048
FF = 768
CAP = 16
AHEAD = 4
NCH = 8
CW = D // NCH
SLOTS = 512
NEAR = 320
BW = 256
NA = 6
U0 = 6
NU = U0 + 2 * NA
QS = ((0, 0), (0, 1), (1, 0), (1, 1))
BLOCKS = tuple(
    [(dy, dz, dc) for dy, dc in QS for dz in (0, -1, 1, -2, 2)]
    + [(dy, -3, dc) for dy, dc in QS]
    + [(dy, 3, dc) for dy, dc in QS]
    + [(0, 4, dc) for dc in (0, 1)]
    + [(1, 4, dc) for dc in (0, 1)]
)


def kernel(
    feat, og, ids_row, gates_row, wg, wu, wd,
    ig_hbm, gg_hbm, dl_hbm,
    ig_out, gg_out, dl_out, out_sem,
    src, mine_meta, msrc, s1, s2, stg1, stg2, stg3, stg4, gs1, gs2, gs3, gs4, rbuf, gbuf,
    wbuf, acc, acts, xt, rg, ret, aa, rp, rm, ysend, yrecv,
    load_sem, w_sem, m_send, m_recv, ring_send, r1, r2, st_send, rx, rx2, gsend, grecv,
    a2_send, d_send, c_send, far_sem, in_sem, y_send, y_sem, ret_send, ret_sem, hop_sem,
):
    rep = lax.axis_index("rep")
    exp = lax.axis_index("exp")
    x = lax.rem(rep, 4)
    yh = rep // 4
    yl = exp // 16
    z = lax.rem(exp // 2, 8)
    c = lax.rem(exp, 2)

    def exp_of(dy, dz, dc):
        return lax.rem(yl + dy, 2) * 16 + lax.rem(z + dz + 8, 8) * 2 + lax.rem(c + dc, 2)

    def near(dy, dz, dc):
        return {"rep": rep, "exp": exp_of(dy, dz, dc)}

    xp = {"rep": yh * 4 + lax.rem(x + 1, 4), "exp": exp}
    xm = {"rep": yh * 4 + lax.rem(x + 3, 4), "exp": exp}
    yo = {"rep": (1 - yh) * 4 + x, "exp": exp}

    def send(a, b, ss, rs, to):
        pltpu.make_async_remote_copy(
            src_ref=a, dst_ref=b, send_sem=ss, recv_sem=rs, device_id=to, device_id_type=MESH
        ).start()

    def local(a, b, sem):
        pltpu.make_async_copy(a, b, sem).start()

    def wait(ref, sem):
        pltpu.make_async_copy(ref, ref, sem).wait()

    def place_of(half, role):
        return lax.rem(yh + 1 + half, 2) * 4 + lax.rem(x + 2 + 3 * role + 3 * (role * (role - 1) // 2), 4)

    def block_of(p):
        return place_of(p // 4, lax.rem(p, 4))

    for k in range(NCH):
        local(feat.at[:, pl.ds(k * CW, CW)], src.at[0, k], load_sem.at[min(k, 1)])
    for k in range(NCH):
        cols = pl.ds(pl.multiple_of(block_of(k) * CW, CW), CW)
        local(og.at[:, cols], src.at[0, NCH + k], load_sem.at[2])
    for m, w in enumerate((wg, wu, wd)):
        local(w.at[0], wbuf.at[m], w_sem.at[m])

    mine_meta[...] = jnp.zeros_like(mine_meta)
    mine_meta[0:2, :] = ids_row[...].astype(F32)
    mine_meta[2:4, :] = gates_row[...].astype(F32)

    up, down = near(0, 1, 0), near(0, -1, 0)
    barrier = pltpu.get_barrier_semaphore()
    peers = [up, down] + [near(dy, 0, dc) for dy, dc in QS[1:]] + [xp, xm, yo]
    for p in peers:
        pl.semaphore_signal(barrier, inc=1, device_id=p, device_id_type=MESH)
    pl.semaphore_wait(barrier, len(peers))

    send(mine_meta, msrc.at[0], m_send.at[0], m_recv.at[0], up)
    send(mine_meta, msrc.at[1], m_send.at[1], m_recv.at[1], down)
    def own_out(k):
        send(src.at[0, k], src.at[1, k], ring_send.at[0], r1.at[k], up)
        send(src.at[0, k], src.at[2, k], ring_send.at[1], r1.at[k], down)

    wait(src.at[0, 0], load_sem.at[0])
    own_out(0)
    wait(src.at[0, pl.ds(1, NCH - 1)], load_sem.at[1])
    for k in range(1, NCH):
        own_out(k)
    wait(src.at[0, pl.ds(NCH, NCH)], load_sem.at[2])

    def greet(i):
        for p in (up, down):
            pl.semaphore_signal(hop_sem.at[i], inc=1, device_id=p, device_id_type=MESH)

    def greeted(i):
        pl.semaphore_wait(hop_sem.at[i], 2)

    greet(0)
    row_i = lax.broadcasted_iota(jnp.int32, (TOK, TOK), 0)
    col_i = lax.broadcasted_iota(jnp.int32, (TOK, TOK), 1)
    before = jnp.where(row_i < col_i, 1.0, 0.0).astype(BF16)
    slot_i = lax.broadcasted_iota(jnp.int32, (CAP, TOK), 0).astype(F32)

    def pick(meta_v, experts):
        i0, i1, g0, g1 = [jnp.broadcast_to(meta_v[i : i + 1, :], (CAP, TOK)) for i in range(4)]
        rows, gates = [], []
        for e in experts:
            ef = e.astype(F32)
            m0, m1 = i0 == ef, i1 == ef
            hit = jnp.where(m0 | m1, 1.0, 0.0)
            pos = jnp.dot(hit.astype(BF16), before, preferred_element_type=F32)
            one = jnp.where(pos == slot_i, hit, 0.0)
            gate = jnp.sum(one * jnp.where(m0, g0, jnp.where(m1, g1, 0.0)), axis=1, keepdims=True)
            rows.append(one.astype(BF16))
            gates.append(jnp.broadcast_to(gate, (CAP, TOK)).astype(BF16))
        return rows, gates

    own_plane = [exp_of(dy, 0, dc) for dy, dc in QS]

    def plan_first(s, meta_v):
        rows, gates = pick(meta_v, own_plane)
        for q in range(4):
            s1[s, pl.ds(q * CAP, CAP), :] = rows[q]
            gs1[q, pl.ds(s * CAP, CAP), :] = gates[q]

    plan_first(0, mine_meta[...])
    wait(msrc.at[0], m_recv.at[0])
    send(msrc.at[0], msrc.at[2], m_send.at[2], m_recv.at[2], up)
    wait(msrc.at[1], m_recv.at[1])
    send(msrc.at[1], msrc.at[3], m_send.at[3], m_recv.at[3], down)
    plan_first(1, msrc[0])
    plan_first(2, msrc[1])
    local(gs1.at[0], gbuf.at[pl.ds(0, 48)], grecv.at[0])
    for q in range(1, 4):
        send(gs1.at[q], gbuf.at[pl.ds(q * 80, 48)], gsend.at[0], grecv.at[0], near(QS[q][0], 0, QS[q][1]))

    def first(k):
        wait(src.at[pl.ds(1, 2), k], r1.at[k])
        send(src.at[1, k], src.at[3, k], ring_send.at[2], r2.at[k], up)
        send(src.at[2, k], src.at[4, k], ring_send.at[3], r2.at[k], down)
        for s in range(3):
            got = jnp.dot(s1[s], src[s, k], preferred_element_type=F32).astype(BF16)
            for q in range(4):
                stg1[q, k, pl.ds(s * CAP, CAP), :] = got[q * CAP : (q + 1) * CAP]
        local(stg1.at[0, k], rbuf.at[k, pl.ds(0, 48)], rx.at[k])
        for q in range(1, 4):
            send(stg1.at[q, k], rbuf.at[k, pl.ds(q * 80, 48)], st_send.at[0], rx.at[k], near(QS[q][0], 0, QS[q][1]))

    def first_x(k, carry):
        first(k)
        return carry

    for i in range(4):
        lax.fori_loop(2 * i, 2 * i + 2, first_x, 0)
        greeted(i)
        if i < 3:
            greet(i + 1)

    for d in range(2):
        step = 1 if d == 0 else -1
        wait(msrc.at[2 + d], m_recv.at[2 + d])
        third = [exp_of(dy, step, dc) for dy, dc in QS]
        fourth = [exp_of(d, 2 * step, dc) for dc in (0, 1)]
        rows, gates = pick(msrc[2 + d], own_plane + third + fourth)
        for i in range(10):
            s2[d, pl.ds(i * CAP, CAP), :] = rows[i]
        for q in range(4):
            gs2[q, pl.ds(d * CAP, CAP), :] = gates[q]
            gs3[d, q] = gates[4 + q]
        for i in range(2):
            gs4[d, i] = gates[8 + i]
    local(gs2.at[0], gbuf.at[pl.ds(48, 32)], grecv.at[0])
    for q in range(1, 4):
        send(gs2.at[q], gbuf.at[pl.ds(q * 80 + 48, 32)], gsend.at[1], grecv.at[0], near(QS[q][0], 0, QS[q][1]))
    for d in range(2):
        step = 1 if d == 0 else -1
        for q in range(4):
            send(gs3.at[d, q], gbuf.at[pl.ds(320 + (d * 4 + q) * CAP, CAP)], gsend.at[2], grecv.at[1], near(QS[q][0], step, QS[q][1]))
        for i in range(2):
            send(gs4.at[d, i], gbuf.at[pl.ds(448 + (d * 2 + i) * CAP, CAP)], gsend.at[3], grecv.at[1], near(d, 2 * step, i))

    def second(k):
        wait(src.at[pl.ds(3, 2), k], r2.at[k])
        for d in range(2):
            step = 1 if d == 0 else -1
            got = jnp.dot(s2[d], src[3 + d, k], preferred_element_type=F32).astype(BF16)
            for q in range(4):
                stg3[d, q, k] = got[(4 + q) * CAP : (5 + q) * CAP]
                stg2[q, k, pl.ds(d * CAP, CAP), :] = got[q * CAP : (q + 1) * CAP]
            for i in range(2):
                stg4[d, i, k] = got[(8 + i) * CAP : (9 + i) * CAP]
        local(stg2.at[0, k], rbuf.at[k, pl.ds(48, 32)], rx.at[k])
        for q in range(1, 4):
            send(stg2.at[q, k], rbuf.at[k, pl.ds(q * 80 + 48, 32)], st_send.at[1], rx.at[k], near(QS[q][0], 0, QS[q][1]))
        for d in range(2):
            step = 1 if d == 0 else -1
            for i in range(2):
                send(stg4.at[d, i, k], rbuf.at[k, pl.ds(448 + (d * 2 + i) * CAP, CAP)], st_send.at[3], rx2.at[k], near(d, 2 * step, i))
            for q in range(4):
                send(stg3.at[d, q, k], rbuf.at[k, pl.ds(320 + (d * 4 + q) * CAP, CAP)], st_send.at[2], rx2.at[k], near(QS[q][0], step, QS[q][1]))

    def second_x(k, carry):
        second(k)
        return carry

    lax.fori_loop(0, NCH, second_x, 0)
    for k in range(AHEAD):
        own_out(NCH + k)

    for m in range(3):
        wait(wbuf.at[m], w_sem.at[m])
    for k in range(NCH):
        wait(rbuf.at[k, pl.ds(0, NEAR)], rx.at[k])

    def near_x(n, carry):
        ncol = pl.ds(pl.multiple_of(n * 256, 256), 256)
        for m in range(2):
            v = jnp.zeros((NEAR, 256), F32)
            for k in range(NCH):
                v = v + jnp.dot(
                    rbuf[k, pl.ds(0, NEAR), :], wbuf[m, pl.ds(k * CW, CW), ncol], preferred_element_type=F32
                )
            acc[m, pl.ds(0, NEAR), ncol] = v
        return carry

    lax.fori_loop(0, FF // 256, near_x, 0)

    def turn_x(k, carry):
        xt[0, k, :, pl.ds(0, 256)] = rbuf[k, pl.ds(0, 256), :].T
        return carry

    lax.fori_loop(0, NCH, turn_x, 0)

    def hidden(i, carry):
        rows = pl.ds(pl.multiple_of(i * 32, 32), 32)
        pg, pu = acc[0, rows, :], acc[1, rows, :]
        sig = jax.nn.sigmoid(pg)
        act = pg * sig
        acts[2, rows, :] = (act * pu).astype(BF16)
        acc[0, rows, :] = pu * sig * (1.0 + pg * (1.0 - sig))
        acc[1, rows, :] = act
        return carry

    lax.fori_loop(0, NEAR // 32, hidden, 0)

    rest = pl.ds(NEAR, SLOTS - NEAR)

    def add_to(m, rows, first_one, part):
        @pl.when(first_one)
        def _():
            acc[m, rows, :] = part

        @pl.when(jnp.logical_not(first_one))
        def _():
            acc[m, rows, :] = acc[m, rows, :] + part

    def far_x(k, carry):
        wait(rbuf.at[k, rest], rx2.at[k])
        krow = pl.ds(pl.multiple_of(k * CW, CW), CW)
        for m in range(2):
            add_to(m, rest, k == 0, jnp.dot(rbuf[k, rest, :], wbuf[m, krow, :], preferred_element_type=F32))
        xt[0, k, :, pl.ds(256, 256)] = rbuf[k, pl.ds(256, 256), :].T
        return carry

    lax.fori_loop(0, NCH // 2, far_x, 0)
    first(NCH)
    first(NCH + 1)
    lax.fori_loop(NCH // 2, NCH, far_x, 0)
    lax.fori_loop(NEAR // 32, SLOTS // 32, hidden, 0)

    def product(role, half, m, cols=slice(None)):
        return jnp.dot(xt[m // 2, place_of(half, role)], acts[m, :, cols], preferred_element_type=F32)

    def put(role, u, v):
        v = v.astype(BF16)
        for i in range(v.shape[1] // BW):
            aa[role, 0, u + i] = v[:TOK, i * BW : (i + 1) * BW]
            aa[role, 1, u + i] = v[TOK:, i * BW : (i + 1) * BW]

    def send_far(u):
        send(aa.at[0, 0, u], rp.at[0, u], a2_send.at[0], far_sem.at[u], xm)
        send(aa.at[0, 1, u], rm.at[0, u], a2_send.at[1], far_sem.at[u], xp)

    def direct_up(u):
        send(aa.at[1, 0, u], rm.at[1, u], d_send.at[0], in_sem.at[u], xp)

    def direct_down(u):
        send(aa.at[2, 1, u], rp.at[1, u], d_send.at[1], in_sem.at[u], xm)

    def direct(u, carry):
        direct_up(u)
        direct_down(u)
        return carry

    def combine(u, carry):
        wait(aa.at[pl.ds(0, 2), 0, u], far_sem.at[u])
        aa[1, 1, u] = (aa[1, 1, u].astype(F32) + rm[0, u].astype(F32)).astype(BF16)
        send(aa.at[1, 1, u], rm.at[2, u], c_send.at[0], in_sem.at[u], xp)
        aa[2, 0, u] = (aa[2, 0, u].astype(F32) + rp[0, u].astype(F32)).astype(BF16)
        send(aa.at[2, 0, u], rp.at[2, u], c_send.at[1], in_sem.at[u], xm)
        return carry

    wait(gbuf.at[pl.ds(0, NEAR)], grecv.at[0])
    wait(gbuf.at[rest], grecv.at[1])

    def turn_dy(p, r0):
        rows = pl.ds(r0, 256)
        g = gbuf[rows, :].astype(F32)
        g = jnp.concatenate([g, g], axis=1)
        xt[1, block_of(p), :, rows] = (g * rbuf[NCH + p, rows, :].astype(F32)).astype(BF16).T

    def down_rows(p):
        return pl.ds(pl.multiple_of(block_of(p) * CW, CW), CW)

    def dy_near(p):
        k = NCH + p
        rows = pl.ds(0, NEAR)
        wait(rbuf.at[k, rows], rx.at[k])
        add_to(2, rows, p == 0, jnp.dot(rbuf[k, rows, :], wbuf[2, down_rows(p), :], preferred_element_type=F32))
        turn_dy(p, 0)

    def dy_far(p):
        k = NCH + p
        wait(rbuf.at[k, rest], rx2.at[k])
        add_to(2, rest, p == 0, jnp.dot(rbuf[k, rest, :], wbuf[2, down_rows(p), :], preferred_element_type=F32))
        turn_dy(p, 256)

    def dy_gradient(p):
        half, role = p // 4, lax.rem(p, 4)
        put(role, half * 3, product(role, half, 2))
        for i in range(3):
            u = half * 3 + i

            @pl.when(role == 0)
            def _():
                send_far(u)

            @pl.when(role == 1)
            def _():
                direct_up(u)

            @pl.when(role == 2)
            def _():
                direct_down(u)

        @pl.when(role == 2)
        def _():
            for i in range(3):
                combine(half * 3 + i, 0)

    def cotangents(j, carry):
        @pl.when(j + AHEAD < NCH)
        def _():
            own_out(NCH + AHEAD + j)

        @pl.when(j + 2 < NCH)
        def _():
            first(NCH + 2 + j)

        second(NCH + j)

        @pl.when(j >= 1)
        def _():
            dy_near(j - 1)

        @pl.when(j >= 2)
        def _():
            dy_far(j - 2)
            dy_gradient(j - 2)

        return carry

    lax.fori_loop(0, NCH, cotangents, 0)

    def pointwise(i, carry):
        rows = pl.ds(pl.multiple_of(i * 32, 32), 32)
        g = gbuf[rows, pl.ds(0, 1)].astype(F32)
        bg = acc[2, rows, :]
        gate = jnp.sum(bg * acts[2, rows, :].astype(F32), axis=1, keepdims=True)
        dh = g * bg
        acts[0, rows, :] = (dh * acc[0, rows, :]).astype(BF16)
        acts[1, rows, :] = (dh * acc[1, rows, :]).astype(BF16)
        rg[rows, pl.ds(D, TOK)] = jnp.broadcast_to(gate, (32, TOK)).astype(BF16)
        return carry

    def back(rows, n):
        nrow = pl.ds(pl.multiple_of(n * 256, 256), 256)
        dims = (((1,), (1,)), ((), ()))
        v = jnp.zeros((rows.size, 256), F32)
        for m in range(2):
            v = v + lax.dot_general(acts[m, rows, :], wbuf[m, nrow, :], dims, preferred_element_type=F32)
        rg[rows, nrow] = v.astype(BF16)

    def back_near(n, carry):
        back(pl.ds(0, NEAR), n)
        return carry

    def back_far(n, carry):
        back(rest, n)
        return carry

    def give_back(lo, hi, dy):
        for i in range(lo, hi):
            rows = pl.ds(i * CAP, CAP)
            if BLOCKS[i] == (0, 0, 0) and dy == 0:
                local(rg.at[rows], ret.at[rows], ret_sem)
            elif BLOCKS[i][0] == dy:
                send(rg.at[rows], ret.at[rows], ret_send, ret_sem, near(*BLOCKS[i]))

    dy_near(NCH - 1)
    lax.fori_loop(0, NEAR // 32, pointwise, 0)
    dy_far(NCH - 2)
    dy_far(NCH - 1)
    lax.fori_loop(NEAR // 32, SLOTS // 32, pointwise, 0)

    def gate_up(role, half):
        u = U0 + half * NA
        put(role, u, product(role, half, 0))
        put(role, u + 3, product(role, half, 1))

    def far_units(half, carry):
        gate_up(0, half)
        for i in range(NA):
            send_far(U0 + half * NA + i)
        return carry

    def beside(half, carry):
        for role in (1, 2):
            gate_up(role, half)
        return carry

    def own(half, carry):
        gate_up(3, half)
        return carry

    def total(u, h):
        s = aa[3, h, u].astype(F32) + rp[2 - h, u].astype(F32)
        return s + rm[1 + h, u].astype(F32)

    def arrived(u):
        wait(aa.at[:, 0, u], in_sem.at[u])

    def across(v, u):
        arrived(u)
        for h in range(2):
            ysend[v, h] = total(u, h).astype(BF16)
        send(ysend.at[v], yrecv.at[v], y_send, y_sem.at[v], yo)

    def across_down(i, carry):
        across(i, i)
        return carry


    def across_rest(i, carry):
        across(3 + i, U0 + i)
        return carry

    lax.fori_loop(0, 1, far_units, 0)
    lax.fori_loop(0, 3, across_down, 0)
    dy_gradient(NCH - 2)
    lax.fori_loop(0, D // 256, back_near, 0)
    give_back(0, NEAR // CAP, 1)
    lax.fori_loop(0, D // 256, back_far, 0)
    give_back(NEAR // CAP, SLOTS // CAP, 1)
    give_back(NEAR // CAP, SLOTS // CAP, 0)
    give_back(0, NEAR // CAP, 0)
    lax.fori_loop(0, 1, beside, 0)
    dy_gradient(NCH - 1)
    lax.fori_loop(U0, U0 + NA, direct, 0)
    lax.fori_loop(U0, U0 + NA, combine, 0)
    lax.fori_loop(1, 2, far_units, 0)
    lax.fori_loop(1, 2, beside, 0)
    lax.fori_loop(U0 + NA, NU, direct, 0)
    lax.fori_loop(0, 2, own, 0)
    lax.fori_loop(0, NA, across_rest, 0)
    lax.fori_loop(U0 + NA, NU, combine, 0)

    lane = lax.broadcasted_iota(jnp.int32, (1, SLOTS), 1)
    blk = lane // CAP
    expert = jnp.zeros((1, SLOTS), F32)
    for i, (dy, dz, dc) in enumerate(BLOCKS):
        expert = jnp.where(blk == i, exp_of(dy, -dz, dc).astype(F32), expert)
    slot = (lane - blk * CAP).astype(F32)
    ids_col = jnp.concatenate([mine_meta[...]] * (TOK // 8), axis=0).T
    h0 = jnp.where(ids_col[:, 0:1] == expert, 1.0, 0.0)
    h1 = jnp.where(ids_col[:, 1:2] == expert, 1.0, 0.0)
    after = jnp.where(row_i > col_i, 1.0, 0.0).astype(BF16)
    pos = jnp.dot(after, (h0 + h1).astype(BF16), preferred_element_type=F32)
    h0 = jnp.where(pos == slot, h0, 0.0).astype(BF16)
    h1 = jnp.where(pos == slot, h1, 0.0).astype(BF16)
    both = h0 + h1
    wait(ret, ret_sem)

    def gather(n, carry):
        ncol = pl.ds(pl.multiple_of(n * 256, 256), 256)
        ig_out[:, ncol] = jnp.dot(both, ret[:, ncol], preferred_element_type=F32).astype(BF16)
        return carry

    lax.fori_loop(0, D // 256, gather, 0)
    local(ig_out, ig_hbm, out_sem.at[0])
    g = ret[:, pl.ds(D, TOK)]
    g0 = jnp.dot(h0, g, preferred_element_type=F32).T
    g1 = jnp.dot(h1, g, preferred_element_type=F32).T
    gg_out[...] = jnp.concatenate([g0[0:1], g1[0:1]], axis=0).astype(BF16)
    local(gg_out, gg_hbm, out_sem.at[1])

    def finish(n, v, u):
        arrived(u)
        wait(yrecv.at[v], y_sem.at[v])
        for h in range(2):
            s = total(u, h) + yrecv[v, h].astype(F32)
            dl_out[n, pl.ds(h * TOK, TOK), :] = (s * 0.125).astype(BF16)
        local(dl_out.at[n], dl_hbm.at[n], out_sem.at[2])

    def finish_down(i, carry):
        finish(6 + i, i, 3 + i)
        return carry

    def finish_rest(i, carry):
        finish(i, 3 + i, U0 + NA + i)
        return carry

    lax.fori_loop(0, 3, finish_down, 0)
    lax.fori_loop(0, NA, finish_rest, 0)

    for i in range(4):
        wait(mine_meta, m_send.at[i])
    wait(stg1.at[pl.ds(1, 3)], st_send.at[0])
    wait(stg2.at[pl.ds(1, 3)], st_send.at[1])
    wait(stg3, st_send.at[2])
    wait(stg4, st_send.at[3])
    wait(gs1.at[pl.ds(1, 3)], gsend.at[0])
    wait(gs2.at[pl.ds(1, 3)], gsend.at[1])
    wait(gs3, gsend.at[2])
    wait(gs4, gsend.at[3])
    for i in range(2):
        wait(src.at[0], ring_send.at[i])
        wait(src.at[1], ring_send.at[2 + i])
        wait(aa.at[0, i], a2_send.at[i])
        wait(aa.at[0, i], d_send.at[i])
        wait(aa.at[0, i], c_send.at[i])
    wait(ysend, y_send)
    wait(rg.at[pl.ds(CAP, SLOTS - CAP)], ret_send)
    wait(ig_out, out_sem.at[0])
    wait(gg_out, out_sem.at[1])
    wait(dl_out, out_sem.at[2])


def place(ig, gg, dl, ig_out, gg_out, dg_out, du_out, dd_out, ig_v, gg_v, dl_v, in_sem, out_sem):
    def copies(out):
        pairs = [(ig, ig_v, ig_out), (gg, gg_v, gg_out)]
        for n in range(9):
            to = (dg_out, du_out, dd_out)[n // 3].at[0, :, pl.ds((n % 3) * BW, BW)]
            pairs.append((dl.at[n], dl_v.at[n], to))
        if out:
            return [pltpu.make_async_copy(v, o, out_sem.at[i]) for i, (_, v, o) in enumerate(pairs)]
        return [pltpu.make_async_copy(a, v, in_sem.at[i]) for i, (a, v, _) in enumerate(pairs)]

    ins, outs = copies(False), copies(True)
    for c in ins:
        c.start()
    for a, b in zip(ins, outs):
        a.wait()
        b.start()
    for c in outs:
        c.wait()


def on_device(features, out_grad, expert_ids, gate_probs, w_gate, w_up, w_down):
    vm, anyspace = pl.BlockSpec(memory_space=pltpu.VMEM), pl.BlockSpec(memory_space=pl.ANY)
    dma = pltpu.SemaphoreType.DMA
    ig, gg, dl = pl.pallas_call(
        kernel,
        name="moe",
        out_shape=(
            jax.ShapeDtypeStruct((TOK, D), BF16),
            jax.ShapeDtypeStruct((2, TOK), BF16),
            jax.ShapeDtypeStruct((9, 256, BW), BF16),
        ),
        in_specs=[anyspace, anyspace, vm, vm, anyspace, anyspace, anyspace],
        out_specs=(anyspace, anyspace, anyspace),
        scratch_shapes=[
            pltpu.VMEM((TOK, D), BF16),
            pltpu.VMEM((2, TOK), BF16),
            pltpu.VMEM((9, 256, BW), BF16),
            dma((3,)),
            pltpu.VMEM((5, 2 * NCH, TOK, CW), BF16),
            pltpu.VMEM((8, TOK), F32),
            pltpu.VMEM((4, 8, TOK), F32),
            pltpu.VMEM((3, 64, TOK), BF16),
            pltpu.VMEM((2, 160, TOK), BF16),
            pltpu.VMEM((4, 2 * NCH, 48, CW), BF16),
            pltpu.VMEM((4, 2 * NCH, 32, CW), BF16),
            pltpu.VMEM((2, 4, 2 * NCH, CAP, CW), BF16),
            pltpu.VMEM((2, 2, 2 * NCH, CAP, CW), BF16),
            pltpu.VMEM((4, 48, TOK), BF16),
            pltpu.VMEM((4, 32, TOK), BF16),
            pltpu.VMEM((2, 4, CAP, TOK), BF16),
            pltpu.VMEM((2, 2, CAP, TOK), BF16),
            pltpu.VMEM((2 * NCH, SLOTS, CW), BF16),
            pltpu.VMEM((SLOTS, TOK), BF16),
            pltpu.VMEM((3, D, FF), BF16),
            pltpu.VMEM((3, SLOTS, FF), F32),
            pltpu.VMEM((3, SLOTS, FF), BF16),
            pltpu.VMEM((2, NCH, CW, SLOTS), BF16),
            pltpu.VMEM((SLOTS, D + TOK), BF16),
            pltpu.VMEM((SLOTS, D + TOK), BF16),
            pltpu.VMEM((4, 2, NU, TOK, BW), BF16),
            pltpu.VMEM((3, NU, TOK, BW), BF16),
            pltpu.VMEM((3, NU, TOK, BW), BF16),
            pltpu.VMEM((3 + NA, 2, TOK, BW), BF16),
            pltpu.VMEM((3 + NA, 2, TOK, BW), BF16),
            dma((3,)),
            dma((3,)),
            dma((4,)),
            dma((4,)),
            dma((4,)),
            dma((2 * NCH,)),
            dma((2 * NCH,)),
            dma((4,)),
            dma((2 * NCH,)),
            dma((2 * NCH,)),
            dma((4,)),
            dma((2,)),
            dma((2,)),
            dma((2,)),
            dma((2,)),
            dma((NU,)),
            dma((NU,)),
            dma,
            dma((3 + NA,)),
            dma,
            dma,
            pltpu.SemaphoreType.REGULAR((4,)),
        ],
        compiler_params=pltpu.CompilerParams(
            collective_id=0, has_side_effects=True, vmem_limit_bytes=67_000_000
        ),
    )(features, out_grad, expert_ids.T, gate_probs.T, w_gate, w_up, w_down)
    delta = jax.ShapeDtypeStruct((1, 256, FF), BF16)
    ig, gg, d_gate, d_up, d_down = pl.pallas_call(
        place,
        name="place",
        out_shape=(
            jax.ShapeDtypeStruct((TOK, D), BF16),
            jax.ShapeDtypeStruct((2, TOK), BF16),
            delta,
            delta,
            delta,
        ),
        in_specs=[anyspace] * 3,
        out_specs=(anyspace,) * 5,
        scratch_shapes=[
            pltpu.VMEM((TOK, D), BF16),
            pltpu.VMEM((2, TOK), BF16),
            pltpu.VMEM((9, 256, BW), BF16),
            dma((11,)),
            dma((11,)),
        ],
    )(ig, gg, dl)
    return (ig, gg.T, d_gate, d_up, d_down)


def solution(mesh):
    rows = P(("rep", "exp"), None)
    weights = P("exp", None, None)
    deltas = P("exp", "rep", None)
    return jax.shard_map(
        on_device,
        mesh=mesh,
        in_specs=(rows, rows, rows, rows, weights, weights, weights),
        out_specs=(rows, rows, deltas, deltas, deltas),
        check_vma=False,
    )
```

time: 161 us -> 150 us (0.932)
  Pallas kernels: 160 us -> 150 us
    pallas_call x1, Pallas kernels: 157 us -> 147 us  [on_device(): pl.pallas_call(kernel, name='moe', out_shape=(jax.ShapeDtypeStruct((TOK,...]
where the time goes in v3:
time: 150 us
  Pallas kernels  150 us (100%)
    pallas_call x1, Pallas kernels, on_device(): pl.pallas_call(kernel, name='moe', out_shape=(jax.ShapeDtypeStruct((TOK,...  147 us

profile of v3, /device:TPU:1, one launch (start us, length us, event | category | flops | bytes accessed | tf_op | source)
XLA Modules:
  0.0 150.4 jit_solution(10715099521816642253)
XLA Ops:
  0.6 147.3 %moe.1 = (bf16[128,2048]{1,0:T(8,128)(2,1)}, bf16[2,128]{1,0:T(2,128)(2,1)}, bf16[9,256,256]{2,1,0:T(8,128)(2,1)}) custom-call(bf16[128,2048]{1,0:T(8,128)(2,1)} %feat.1, bf16[128,2048]{1,0:T(8,128)(2,1)} %og.1, s32[2,128]{1,0:T(2,128)} %bitcast.3, bf16[2,128]{1,0:T(2,128)(2,1)} %bitcast.4, bf16[1,2048,768]{2,1,0:T(8,128)(2,1)} %wg.1, ...), custom_call_target="tpu_custom_call" | custom-call | tf_op jit(solution)/shard_map/moe/pallas_call | solution.py:593
  147.9 2.4 %place.1 = (bf16[128,2048]{1,0:T(8,128)(2,1)}, bf16[2,128]{1,0:T(2,128)(2,1)}, bf16[1,256,768]{2,1,0:T(8,128)(2,1)}, bf16[1,256,768]{2,1,0:T(8,128)(2,1)}, bf16[1,256,768]{2,1,0:T(8,128)(2,1)}) custom-call(bf16[128,2048]{1,0:T(8,128)(2,1)} %get-tuple-element.13.ig, bf16[2,128]{1,0:T(2,128)(2,1)} %get-tuple-element.14.gg, ...), custom_call_target="tpu_custom_call" | custom-call | tf_op jit(solution)/shard_map/place/pallas_call | solution.py:662

commit v4 on v3

--- a/solution.py
+++ b/solution.py
@@ -74,8 +74,12 @@
     def place_of(half, role):
         return lax.rem(yh + 1 + half, 2) * 4 + lax.rem(x + 2 + 3 * role + 3 * (role * (role - 1) // 2), 4)
 
+    def part_of(p):
+        own = p // 6
+        return own * (p - 6) + (1 - own) * (p // 3), own * 3 + (1 - own) * lax.rem(p, 3)
+
     def block_of(p):
-        return place_of(p // 4, lax.rem(p, 4))
+        return place_of(*part_of(p))
 
     for k in range(NCH):
         local(feat.at[:, pl.ds(k * CW, CW)], src.at[0, k], load_sem.at[min(k, 1)])
@@ -347,7 +351,7 @@
         turn_dy(p, 256)
 
     def dy_gradient(p):
-        half, role = p // 4, lax.rem(p, 4)
+        half, role = part_of(p)
         put(role, half * 3, product(role, half, 2))
         for i in range(3):
             u = half * 3 + i
@@ -364,10 +368,10 @@
             def _():
                 direct_down(u)
 
-        @pl.when(role == 2)
+        @pl.when(p == 2)
         def _():
             for i in range(3):
-                combine(half * 3 + i, 0)
+                combine(i, 0)
 
     def cotangents(j, carry):
         @pl.when(j + AHEAD < NCH)
@@ -477,14 +481,15 @@
         return carry
 
     lax.fori_loop(0, 1, far_units, 0)
+    dy_gradient(NCH - 2)
     lax.fori_loop(0, 3, across_down, 0)
-    dy_gradient(NCH - 2)
     lax.fori_loop(0, D // 256, back_near, 0)
     give_back(0, NEAR // CAP, 1)
     lax.fori_loop(0, D // 256, back_far, 0)
     give_back(NEAR // CAP, SLOTS // CAP, 1)
     give_back(NEAR // CAP, SLOTS // CAP, 0)
     give_back(0, NEAR // CAP, 0)
+    lax.fori_loop(3, 6, combine, 0)
     lax.fori_loop(0, 1, beside, 0)
     dy_gradient(NCH - 1)
     lax.fori_loop(U0, U0 + NA, direct, 0)

time: 150 us -> 148 us (0.987)
  Pallas kernels: 150 us -> 147 us
    pallas_call x1, Pallas kernels: 147 us -> 145 us  [on_device(): pl.pallas_call(kernel, name='moe', out_shape=(jax.ShapeDtypeStruct((TOK,...]
where the time goes in v4:
time: 148 us
  Pallas kernels  147 us (99%)
    pallas_call x1, Pallas kernels, on_device(): pl.pallas_call(kernel, name='moe', out_shape=(jax.ShapeDtypeStruct((TOK,...  145 us

profile of v4, /device:TPU:1, one launch (start us, length us, event | category | flops | bytes accessed | tf_op | source)
XLA Modules:
  0.0 147.9 jit_solution(8594404104728312222)
XLA Ops:
  0.6 144.8 %moe.1 = (bf16[128,2048]{1,0:T(8,128)(2,1)}, bf16[2,128]{1,0:T(2,128)(2,1)}, bf16[9,256,256]{2,1,0:T(8,128)(2,1)}) custom-call(bf16[128,2048]{1,0:T(8,128)(2,1)} %feat.1, bf16[128,2048]{1,0:T(8,128)(2,1)} %og.1, s32[2,128]{1,0:T(2,128)} %bitcast.3, bf16[2,128]{1,0:T(2,128)(2,1)} %bitcast.4, bf16[1,2048,768]{2,1,0:T(8,128)(2,1)} %wg.1, ...), custom_call_target="tpu_custom_call" | custom-call | tf_op jit(solution)/shard_map/moe/pallas_call | solution.py:598
  145.5 2.4 %place.1 = (bf16[128,2048]{1,0:T(8,128)(2,1)}, bf16[2,128]{1,0:T(2,128)(2,1)}, bf16[1,256,768]{2,1,0:T(8,128)(2,1)}, bf16[1,256,768]{2,1,0:T(8,128)(2,1)}, bf16[1,256,768]{2,1,0:T(8,128)(2,1)}) custom-call(bf16[128,2048]{1,0:T(8,128)(2,1)} %get-tuple-element.13.ig, bf16[2,128]{1,0:T(2,128)(2,1)} %get-tuple-element.14.gg, ...), custom_call_target="tpu_custom_call" | custom-call | tf_op jit(solution)/shard_map/place/pallas_call | solution.py:667

commit v5 on v4

--- a/solution.py
+++ b/solution.py
@@ -289,8 +289,8 @@
 
     lax.fori_loop(0, NCH // 2, far_x, 0)
     first(NCH)
+    lax.fori_loop(NCH // 2, NCH, far_x, 0)
     first(NCH + 1)
-    lax.fori_loop(NCH // 2, NCH, far_x, 0)
     lax.fori_loop(NEAR // 32, SLOTS // 32, hidden, 0)
 
     def product(role, half, m, cols=slice(None)):

time: 148 us -> 151 us (1.020); the launches traced: 148 us -> 148 us
  no operation moved by 1% of the time
where the time goes in v5:
time: 151 us; the launch traced here: 148 us
  Pallas kernels  147 us (97%)
    pallas_call x1, Pallas kernels, on_device(): pl.pallas_call(kernel, name='moe', out_shape=(jax.ShapeDtypeStruct((TOK,...  145 us

profile of v5, /device:TPU:1, one launch (start us, length us, event | category | flops | bytes accessed | tf_op | source)
XLA Modules:
  0.0 147.6 jit_solution(14663742992739919776)
XLA Ops:
  0.6 144.6 %moe.1 = (bf16[128,2048]{1,0:T(8,128)(2,1)}, bf16[2,128]{1,0:T(2,128)(2,1)}, bf16[9,256,256]{2,1,0:T(8,128)(2,1)}) custom-call(bf16[128,2048]{1,0:T(8,128)(2,1)} %feat.1, bf16[128,2048]{1,0:T(8,128)(2,1)} %og.1, s32[2,128]{1,0:T(2,128)} %bitcast.3, bf16[2,128]{1,0:T(2,128)(2,1)} %bitcast.4, bf16[1,2048,768]{2,1,0:T(8,128)(2,1)} %wg.1, ...), custom_call_target="tpu_custom_call" | custom-call | tf_op jit(solution)/shard_map/moe/pallas_call | solution.py:598
  145.2 2.4 %place.1 = (bf16[128,2048]{1,0:T(8,128)(2,1)}, bf16[2,128]{1,0:T(2,128)(2,1)}, bf16[1,256,768]{2,1,0:T(8,128)(2,1)}, bf16[1,256,768]{2,1,0:T(8,128)(2,1)}, bf16[1,256,768]{2,1,0:T(8,128)(2,1)}) custom-call(bf16[128,2048]{1,0:T(8,128)(2,1)} %get-tuple-element.13.ig, bf16[2,128]{1,0:T(2,128)(2,1)} %get-tuple-element.14.gg, ...), custom_call_target="tpu_custom_call" | custom-call | tf_op jit(solution)/shard_map/place/pallas_call | solution.py:667
